TPU v7x, 32 devices: a whole 2x2x4 slice. The times are simulated.
32 devices in a mesh: expert: 4 (over x, core), shard: 8 (over z, y).
Axes of the slice: x: 2, y: 2, z: 4, core: 2. Of those that a mesh axis runs over, the one named last changes fastest.
Arguments:
- tokens_in: bfloat16 [1024, 4096], P(('expert', 'shard')), may hold values from -6 to 6
- out_grad: bfloat16 [1024, 2, 8192], P(('expert', 'shard')), may hold values from -6 to 6
- expert_ids: int32 [1024, 2], P(('expert', 'shard')), may hold values from 0 to 3, all different within a row; in each aligned block of 32 rows (0 to 31, 32 to 63, ...) at most 20 rows name the same one
- d_levels: int32 [4, 16], P('expert'), may hold values from 0 to 7
- f_levels: int32 [4, 32], P('expert', 'shard'), may hold values from 0 to 7
Outputs:
- ascent: bfloat16 [4, 4096, 8192], P('expert', None, 'shard')
Inputs may be any that keep to these rules, and one draw needn't show every extreme that they name: `expert_ids`: each token names two different experts; among the 64 entries of one device no expert is named more than 20 times, and 20 is reached on some device; every expert is named somewhere.
All inputs are finite; a program needn't handle non-finite values.
Results may differ from a plain program's by a relative error of at most 0.001.
Values may be sent and summed in bfloat16 or wider, within the bound.
A program may use at most 128 MiB of HBM per device.

v0:
```python
import functools

import jax
import jax.numpy as jnp
from jax import lax
from jax.experimental import pallas as pl
from jax.experimental.pallas import tpu as pltpu
from jax.sharding import PartitionSpec as P

BLK = 256
HALF = BLK // 2
MARK = 128
NT = (((1,), (1,)), ((), ()))
TN = (((0,), (0,)), ((), ()))


def dot_f32(a, b, dims=(((1,), (0,)), ((), ()))):
    return lax.dot_general(
        a, b, dims, precision=lax.Precision.HIGHEST, preferred_element_type=jnp.float32
    )


def dot_bf16(a, b, dims=(((1,), (0,)), ((), ()))):
    return lax.dot_general(a, b, dims, preferred_element_type=jnp.float32)


def split(value, parts):
    out = []
    for _ in range(parts):
        part = value.astype(jnp.bfloat16)
        out.append(part)
        value = value - part.astype(jnp.float32)
    return out


def gauss_jordan(work, count):
    lanes = lax.broadcasted_iota(jnp.int32, (HALF, HALF), 1)
    lane_row = lax.broadcasted_iota(jnp.int32, (1, HALF), 1)

    def step(j, carry):
        index = jnp.full((HALF, HALF), j, jnp.int32)
        at_pivot = lanes == j
        matrices = [work[b] for b in range(count)]
        rows = [work[b, pl.ds(j, 1), :] for b in range(count)]
        pivots = [
            jnp.sum(jnp.where(lane_row == j, row, 0.0), axis=1, keepdims=True) for row in rows
        ]
        columns = [jnp.take_along_axis(matrix, index, axis=1) for matrix in matrices]
        scaled = [
            jnp.where(lane_row == j, 1.0, row) / pivot for row, pivot in zip(rows, pivots)
        ]
        updated = [
            jnp.where(at_pivot, 0.0, matrix) - column * row
            for matrix, column, row in zip(matrices, columns, scaled)
        ]
        for b in range(count):
            work[b] = updated[b]
        for b in range(count):
            work[b, pl.ds(j, 1), :] = scaled[b]
        return carry

    lax.fori_loop(0, HALF, step, 0)


def invert_covariances(rows_ref, damp_ref, count_ref, work, cov, aux):
    count = cov.shape[0]
    eye = (
        lax.broadcasted_iota(jnp.int32, (BLK, BLK), 0)
        == lax.broadcasted_iota(jnp.int32, (BLK, BLK), 1)
    )
    for b in range(count):
        rows = rows_ref[:, b * BLK : (b + 1) * BLK]
        product = dot_bf16(rows, rows, TN) / count_ref[0]
        cov[b] = product + jnp.where(eye, damp_ref[b], 0.0)
        work[b] = cov[b, :HALF, :HALF]
    gauss_jordan(work, count)
    for b in range(count):
        first = work[b]
        upper = cov[b, :HALF, HALF:]
        side = dot_f32(first, upper)
        aux[b] = side
        cov[b, :HALF, :HALF] = first
        work[b] = cov[b, HALF:, HALF:] - dot_f32(upper, side, TN)
    gauss_jordan(work, count)
    for b in range(count):
        last = work[b]
        side = aux[b]
        corner = dot_f32(side, last)
        cov[b, :HALF, :HALF] = cov[b, :HALF, :HALF] + dot_f32(corner, side, NT)
        cov[b, :HALF, HALF:] = -corner
        cov[b, HALF:, :HALF] = -corner.T
        cov[b, HALF:, HALF:] = last


def input_kernel(damp_ref, count_ref, rows_ref, inv_ref, work, aux):
    invert_covariances(rows_ref, damp_ref, count_ref, work, inv_ref, aux)


def hidden_kernel(damp_ref, count_ref, rows_ref, high_ref, low_ref, work, aux, cov):
    invert_covariances(rows_ref, damp_ref, count_ref, work, cov, aux)
    for b in range(cov.shape[0]):
        columns = slice(b * BLK, (b + 1) * BLK)
        rows = rows_ref[:, columns]
        total = sum(dot_bf16(rows, part) for part in reversed(split(cov[b], 3)))
        high_ref[:, columns], low_ref[:, columns] = split(total, 2)


def product_kernel(rows_ref, inv_ref, high_ref, low_ref, out_ref, norm_ref):
    rows = rows_ref[0]
    left = sum(dot_bf16(part, rows, NT) for part in reversed(split(inv_ref[0], 3)))
    left_high, left_low = split(left, 2)
    high = high_ref[...]
    out = dot_bf16(left_high, low_ref[...]) + dot_bf16(left_low, high) + dot_bf16(left_high, high)
    out_ref[...] = out

    @pl.when(pl.program_id(0) == 0)
    def _():
        norm_ref[...] = jnp.zeros_like(norm_ref)

    norm_ref[...] += jnp.sum((out * out).reshape(-1, 8, out.shape[1]), axis=0)


def damping(levels):
    return 0.05 * jnp.exp(0.4 * levels.astype(jnp.float32))


def call_blocks(kernel, damp, row_count, rows, out_shape, with_cov):
    count = damp.shape[0]
    scratch = [pltpu.VMEM((count, HALF, HALF), jnp.float32)] * 2
    if with_cov:
        scratch.append(pltpu.VMEM((count, BLK, BLK), jnp.float32))
    vmem = pl.BlockSpec(memory_space=pltpu.VMEM)
    smem = pl.BlockSpec(memory_space=pltpu.SMEM)
    return pl.pallas_call(
        kernel,
        out_shape=out_shape,
        in_specs=[smem, smem, vmem],
        out_specs=jax.tree.map(lambda _: vmem, out_shape),
        scratch_shapes=scratch,
        compiler_params=pltpu.CompilerParams(vmem_limit_bytes=48 << 20),
        cost_estimate=pl.CostEstimate(flops=20_000_000_000, bytes_accessed=4_000_000, transcendentals=0),
    )(damp, row_count, rows)


def local(tokens_in, out_grad, expert_ids, d_levels, f_levels):
    group_count = lax.axis_size("expert")
    shard_count = lax.axis_size("shard")
    tok_rows = tokens_in.shape[0]
    width = tokens_in.shape[1]
    ff_full = out_grad.shape[2]
    ff_dev = ff_full // shard_count
    width_dev = width // shard_count
    capacity = min(tok_rows, max(2, 5 * tok_rows // (2 * group_count)))
    slot_total = group_count * capacity
    flat_ids = expert_ids.reshape(-1)
    member = (flat_ids[:, None] == jnp.arange(group_count, dtype=jnp.int32)[None, :]).astype(
        jnp.int32
    )
    before = jnp.cumsum(member, axis=0) - member
    ranking = jnp.sum(before * member, axis=1)
    target = flat_ids * capacity + ranking
    dispatch = (jnp.arange(slot_total, dtype=jnp.int32)[:, None] == target[None, :]).astype(
        jnp.bfloat16
    )
    per_token = jnp.sum(
        dispatch.reshape(slot_total, tok_rows, 2).astype(jnp.float32), axis=2
    ).astype(jnp.bfloat16)
    x_send = jnp.dot(per_token, tokens_in, preferred_element_type=jnp.float32).astype(jnp.bfloat16)
    g_send = jnp.dot(
        dispatch, out_grad.reshape(2 * tok_rows, ff_full), preferred_element_type=jnp.float32
    ).astype(jnp.bfloat16)
    valid_slot = jnp.sum(dispatch.astype(jnp.float32), axis=1).astype(jnp.bfloat16)
    send = jnp.concatenate(
        (
            x_send.reshape(group_count, capacity, shard_count, width_dev),
            g_send.reshape(group_count, capacity, shard_count, ff_dev),
            jnp.broadcast_to(
                valid_slot.reshape(group_count, capacity, 1, 1),
                (group_count, capacity, shard_count, MARK),
            ),
        ),
        axis=3,
    )
    send = send.transpose(0, 2, 1, 3).reshape(group_count * shard_count, capacity, -1)
    rows = lax.all_to_all(send, ("expert", "shard"), split_axis=0, concat_axis=0, tiled=True)
    rows = rows.reshape(-1, rows.shape[2])
    own_x = rows[:, :width_dev]
    rows_g = rows[:, width_dev : width_dev + ff_dev]
    row_count = jnp.sum(rows[:, width_dev + ff_dev].astype(jnp.float32)).reshape(1)
    row_total = rows.shape[0]
    rows_x = lax.all_gather(own_x, "shard", axis=0)

    own_blocks = width_dev // BLK
    first_block = lax.axis_index("shard") * own_blocks
    own_levels = lax.dynamic_slice_in_dim(d_levels[0], first_block, own_blocks, 0)
    inv_a = call_blocks(
        input_kernel,
        damping(own_levels),
        row_count,
        own_x,
        jax.ShapeDtypeStruct((own_blocks, BLK, BLK), jnp.float32),
        False,
    )
    inv_a = lax.all_gather(inv_a, "shard", axis=0, tiled=True)
    half = jax.ShapeDtypeStruct((row_total, ff_dev), jnp.bfloat16)
    g_high, g_low = call_blocks(
        hidden_kernel, damping(f_levels[0]), row_count, rows_g, (half, half), True
    )
    blocks = width // BLK
    whole = pl.BlockSpec((row_total, ff_dev), lambda b: (0, 0))
    precond, squares = pl.pallas_call(
        product_kernel,
        grid=(blocks,),
        out_shape=(
            jax.ShapeDtypeStruct((width, ff_dev), jnp.float32),
            jax.ShapeDtypeStruct((8, ff_dev), jnp.float32),
        ),
        in_specs=[
            pl.BlockSpec((1, row_total, BLK), lambda b: (b // own_blocks, 0, b % own_blocks)),
            pl.BlockSpec((1, BLK, BLK), lambda b: (b, 0, 0)),
            whole,
            whole,
        ],
        out_specs=(
            pl.BlockSpec((BLK, ff_dev), lambda b: (b, 0)),
            pl.BlockSpec((8, ff_dev), lambda b: (0, 0)),
        ),
        compiler_params=pltpu.CompilerParams(
            dimension_semantics=("arbitrary",), vmem_limit_bytes=48 << 20
        ),
        cost_estimate=pl.CostEstimate(
            flops=6 * row_total * width * ff_dev, bytes_accessed=4 * width * ff_dev, transcendentals=0
        ),
    )(rows_x, inv_a, g_high, g_low)
    norm_total = lax.psum(jnp.sum(squares), ("expert", "shard"))
    ascent_scale = lax.rsqrt(norm_total / (group_count * width * ff_full) + 1e-06)
    return (precond * ascent_scale).astype(jnp.bfloat16)[None]


def solution(mesh):
    return jax.shard_map(
        local,
        mesh=mesh,
        in_specs=(
            P(("expert", "shard"), None),
            P(("expert", "shard"), None, None),
            P(("expert", "shard"), None),
            P("expert", None),
            P("expert", "shard"),
        ),
        out_specs=P("expert", None, "shard"),
        check_vma=False,
    )
```

profile of v0, /device:TPU:0, one launch (start us, length us, event | category | flops | bytes accessed | tf_op | source)
XLA Modules:
  0.0 371.0 jit_solution(4334765578300746740)
XLA Ops:
  6.5 0.0 copy-start
  6.5 0.0 copy-start.2
  6.5 0.9 copy.23
  7.4 0.1 eq.36
  7.5 0.1 fusion.2
  7.6 0.1 reduce_window_sum.11
  7.7 0.2 select_reduce_fusion
  7.9 0.1 reduce_sum.54
  8.0 0.1 fusion.5
  8.1 0.1 broadcast_in_dim.6
  8.2 0.1 copy.24
  8.2 0.7 multiply_add_fusion
  8.9 0.1 fusion.4
  9.0 0.0 copy-done
  9.0 0.3 convolution_convert_fusion.1
  9.4 0.2 copy.26
  9.6 0.0 copy-done.2
  9.6 0.4 reshape.55
  10.1 0.6 convolution_convert_fusion
  10.7 0.8 copy.27
  11.5 0.1 broadcast_in_dim.14
  11.6 0.2 maximum_bitcast_fusion
  11.8 1.8 copy.25
  13.6 0.0 copy-start.3
  13.6 7.3 %all-to-all-start = ((bf16[32,20,1664]{2,1,0:T(8,128)(2,1)}), bf16[32,20,1664]{2,1,0:T(8,128)(2,1)S(1)}, u32[]{:S(2)}, u32[]{:S(2)}) async-start(bf16[32,20,1664]{2,1,0:T(8,128)(2,1)} %bitcast.20), calls=%async_computation | async-start | bytes 5111808 | tf_op jit(solution)/shard_map/all_to_all | solution.py:185
  20.9 0.0 all-gather.4.cloned.1.call-start
  20.9 0.0 copy-done.3
  21.0 0.1 multiply_bitcast_fusion.1.damp_ref
  21.0 59.9 %all-to-all-done = bf16[32,20,1664]{2,1,0:T(8,128)(2,1)S(1)} async-done(((bf16[32,20,1664]{2,1,0:T(8,128)(2,1)}), bf16[32,20,1664]{2,1,0:T(8,128)(2,1)S(1)}, u32[]{:S(2)}, u32[]{:S(2)}) %all-to-all-start) | async-done | bytes 2129952 | tf_op jit(solution)/shard_map/all_to_all | solution.py:185
  81.0 2.0 reshape.58
  82.9 1.7 convert_reduce_fusion
  84.6 1.1 slice.12.rows_ref
  85.7 0.0 copy-start.1
  85.8 0.0 copy-start.4
  85.8 40.0 %shard_map.55 = f32[2,256,256]{2,1,0:T(8,128)} custom-call(f32[2]{0:T(128)S(1)} %multiply_bitcast_fusion.1.damp_ref, f32[1]{0:T(128)} %bitcast.4.count_ref, bf16[640,512]{1,0:T(8,128)(2,1)S(1)} %slice.12.rows_ref), custom_call_target="tpu_custom_call" | custom-call | flops 20000000000 | bytes 4000000 | tf_op jit(solution)/shard_map/pallas_call | solution.py:134
  125.8 0.0 copy-done.1
  125.8 0.0 all-gather.4.cloned.1.call-update
  125.8 0.0 all-gather.6.cloned.1.call-start
  125.9 0.7 all-gather.6.cloned.1.call-update
  126.6 0.0 copy-done.4
  126.6 1.4 slice.14.rows_ref
  128.0 52.2 %shard_map.56 = (bf16[640,1024]{1,0:T(8,128)(2,1)S(1)}, bf16[640,1024]{1,0:T(8,128)(2,1)S(1)}) custom-call(f32[4]{0:T(128)S(1)} %multiply_bitcast_fusion.damp_ref, f32[1]{0:T(128)} %bitcast.4.count_ref, bf16[640,1024]{1,0:T(8,128)(2,1)S(1)} %slice.14.rows_ref), custom_call_target="tpu_custom_call" | custom-call | flops 20000000000 | bytes 4000000 | tf_op jit(solution)/shard_map/pallas_call | solution.py:134
  180.2 16.4 %all-gather.4.cloned.1.call-done.inv_ref = f32[16,256,256]{2,1,0:T(8,128)} async-done(((f32[2,256,256]{2,1,0:T(8,128)}), f32[16,256,256]{2,1,0:T(8,128)}) %all-gather.4.cloned.1.call-update) | async-done | bytes 4194320 | tf_op jit(solution)/shard_map/all_gather | solution.py:204
  196.6 86.6 %all-gather.6.cloned.1.call-done = bf16[5120,512]{1,0:T(8,128)(2,1)} async-done(((bf16[640,512]{1,0:T(8,128)(2,1)}), bf16[5120,512]{1,0:T(8,128)(2,1)}) %all-gather.6.cloned.1.call-update) | async-done | bytes 5242896 | tf_op jit(solution)/shard_map/all_gather | solution.py:191
  283.2 31.5 %shard_map.57 = (f32[4096,1024]{1,0:T(8,128)}, f32[8,1024]{1,0:T(8,128)S(1)}) custom-call(bf16[8,640,512]{2,1,0:T(8,128)(2,1)} %bitcast.25, f32[16,256,256]{2,1,0:T(8,128)} %all-gather.4.cloned.1.call-done.inv_ref, bf16[640,1024]{1,0:T(8,128)(2,1)S(1)} %get-tuple-element.9.high_ref, bf16[640,1024]{1,0:T(8,128)(2,1)S(1)} %get-tuple-element.10.low_ref), custom_call_target="tpu_custom_call" | custom-call | flops 16106127360 | bytes 16777216 | tf_op jit(solution)/shard_map/pallas_call | solution.py:211
  314.7 0.6 reduce_sum.58
  315.3 38.6 %psum.7 = f32[]{:T(128)} all-reduce(f32[]{:T(128)} %reduce_sum.58), channel_id=1, replica_groups=mesh['expert'=4,'shard'=8] {'expert','shard'}, use_global_device_ids=true, to_apply=%region_6.7 | all-reduce | flops 1 | bytes 8 | tf_op jit(solution)/shard_map/psum | solution.py:235
  354.6 9.6 %fusion = bf16[1,4096,1024]{2,1,0:T(8,128)(2,1)} fusion(f32[4096,1024]{1,0:T(8,128)} %get-tuple-element.11, f32[]{:T(128)S(6)} %rsqrt.3), kind=kLoop, calls=%fused_computation.2 | loop fusion | flops 8388608 | bytes 25165828 | tf_op jit(solution)/shard_map/broadcast_in_dim | solution.py:237
  (2 shorter events, 0.0 us)
Async XLA Ops:
  6.5 2.5 copy-start
  6.5 3.1 copy-start.2
  13.6 7.4 %copy-start.3 = (s32[1,16]{1,0:T(1,128)S(1)}, s32[1,16]{1,0:T(1,128)}, u32[]{:S(2)}) copy-start(s32[1,16]{1,0:T(1,128)} %param.8) | copy-start | bytes 196
  13.6 67.4 %all-to-all-start = ((bf16[32,20,1664]{2,1,0:T(8,128)(2,1)}), bf16[32,20,1664]{2,1,0:T(8,128)(2,1)S(1)}, u32[]{:S(2)}, u32[]{:S(2)}) async-start(bf16[32,20,1664]{2,1,0:T(8,128)(2,1)} %bitcast.20), calls=%async_computation | async-start | bytes 5111808 | tf_op jit(solution)/shard_map/all_to_all | solution.py:185
  20.9 175.7 %all-gather.4.cloned.1.call-start = ((), (), s32[]{:S(2)}) async-start(), calls=%async_computation.1 | async-start | bytes 4718592 | tf_op jit(solution)/shard_map/all_gather | solution.py:204
  85.7 40.1 %copy-start.1 = (bf16[640,512]{1,0:T(8,128)(2,1)}, bf16[640,512]{1,0:T(8,128)(2,1)S(1)}, u32[]{:S(2)}) copy-start(bf16[640,512]{1,0:T(8,128)(2,1)S(1)} %slice.12.rows_ref) | copy-start | bytes 1966084
  85.8 40.8 %copy-start.4 = (s32[1,4]{1,0:T(1,128)S(1)}, s32[1,4]{1,0:T(1,128)}, u32[]{:S(2)}) copy-start(s32[1,4]{1,0:T(1,128)} %param.9) | copy-start | bytes 52
  125.8 157.4 %all-gather.6.cloned.1.call-start = ((), (), s32[]{:S(2)}) async-start(), calls=%async_computation.2 | async-start | bytes 5898240 | tf_op jit(solution)/shard_map/all_gather | solution.py:191
Sparse Core Ops, SparseCore 0:
  126.0 70.5 all-gather.3
  198.7 84.4 all-gather.5
where the time goes:
time: 371 us
  waiting for transfers between devices  164 us (44%)
  Pallas kernels  124 us (33%)
  blocking collectives  38.6 us (10%)
  between operations  14.3 us (4%)
  other arithmetic  13.4 us (4%)
  local copies, waits for them, and re-layouts  9.13 us (2%)
  starting transfers between devices  7.41 us (2%)
    pallas_call x2, Pallas kernels, call_blocks(): pl.pallas_call(kernel, out_shape=out_shape, in_specs=[smem, smem, vmem],...  92.2 us
    all_gather x1, waiting for transfers between devices, local(): rows_x = lax.all_gather(own_x, 'shard', axis=0)  86.6 us
    all_to_all x1, waiting for transfers between devices, local(): lax.all_to_all(send, ('expert', 'shard'), split_axis=0, concat_axis=0, ti...  59.9 us
    psum x1, blocking collectives, local(): norm_total = lax.psum(jnp.sum(squares), ('expert', 'shard'))  38.6 us
    pallas_call x1, Pallas kernels, local(): pl.pallas_call(product_kernel, grid=(blocks,), out_shape=(jax.ShapeDtypeS...  31.5 us
    all_gather x1, waiting for transfers between devices, local(): inv_a = lax.all_gather(inv_a, 'shard', axis=0, tiled=True)  16.4 us
    broadcast_in_dim x1, other arithmetic, local(): return (precond * ascent_scale).astype(jnp.bfloat16)[None]  9.6 us
  transfers between devices with their start and end apart: 3, of which 3 were waited for; matrix products, arithmetic and copies ran while one was open for 0% of the time, Pallas kernels for 14%

commit v1 on v0

--- a/solution.py
+++ b/solution.py
@@ -10,6 +10,8 @@
 BLK = 256
 HALF = BLK // 2
 MARK = 128
+MESH = pl.DeviceIdType.MESH
+NN = (((1,), (0,)), ((), ()))
 NT = (((1,), (1,)), ((), ()))
 TN = (((0,), (0,)), ((), ()))
 
@@ -142,7 +144,7 @@
     )(damp, row_count, rows)
 
 
-def local(tokens_in, out_grad, expert_ids, d_levels, f_levels):
+def plain(tokens_in, out_grad, expert_ids, d_levels, f_levels):
     group_count = lax.axis_size("expert")
     shard_count = lax.axis_size("shard")
     tok_rows = tokens_in.shape[0]
@@ -237,6 +239,533 @@
     return (precond * ascent_scale).astype(jnp.bfloat16)[None]
 
 
+def comm_kernel(group, shards, pair, x_ref, m_ref, xall, rall, zs, ys, xs, ps, gs, xr, gr, local):
+    expert = lax.axis_index("expert")
+    shard = lax.axis_index("shard")
+    chip_x, core = expert // 2, lax.rem(expert, 2)
+    depth = shards // pair
+    z, y = shard // pair, lax.rem(shard, pair)
+    cols = xall.shape[3]
+    me = expert * shards + shard
+
+    def place(px, py, pz, pc):
+        return (px * 2 + pc, pz * pair + py)
+
+    def number(px, py, pz, pc):
+        return (px * 2 + pc) * shards + pz * pair + py
+
+    others = [
+        (lax.rem(expert + de, group), lax.rem(shard + ds, shards))
+        for ds in range(shards)
+        for de in range(group)
+        if de or ds
+    ]
+    barrier = pltpu.get_barrier_semaphore()
+    for other in others:
+        pl.semaphore_signal(barrier, 1, device_id=other, device_id_type=MESH)
+    pl.semaphore_wait(barrier, len(others))
+
+    pending = []
+
+    def send(valid, source, unit, half, target, sem):
+        copy = pltpu.make_async_remote_copy(
+            src_ref=source,
+            dst_ref=xall.at[half, unit],
+            send_sem=sem,
+            recv_sem=xr.at[unit * 2 + half],
+            device_id=target,
+            device_id_type=MESH,
+        )
+        pl.when(valid)(copy.start)
+        pending.append((valid, copy))
+
+    def arrive(valid, unit, half):
+        @pl.when(valid)
+        def _():
+            pltpu.make_async_remote_copy(
+                src_ref=xall.at[half, unit],
+                dst_ref=xall.at[half, unit],
+                send_sem=zs.at[0],
+                recv_sem=xr.at[unit * 2 + half],
+                device_id=(expert, shard),
+                device_id_type=MESH,
+            ).wait_recv()
+
+    def along_z(valid, up, k, half):
+        origin = z - k if up else z + k
+        unit = number(chip_x, y, origin, core)
+        source = x_ref.at[:, pl.ds(half * cols, cols)] if k == 0 else xall.at[half, unit]
+        more = jnp.logical_and(valid, z < depth - 1 if up else z > 0)
+        step = 1 if up else -1
+        send(more, source, unit, half, place(chip_x, y, z + step, core), zs.at[(k * 2 + half) * 2 + int(up)])
+
+    def spread(valid, origin, k, half):
+        unit = number(chip_x, y, origin, core)
+        source = x_ref.at[:, pl.ds(half * cols, cols)] if k == 0 else xall.at[half, unit]
+        send(valid, source, unit, half, place(chip_x, 1 - y, z, core), ys.at[origin * 2 + half])
+        send(valid, source, unit, half, place(1 - chip_x, y, z, core), xs.at[origin * 2 + half])
+        send(valid, source, unit, half, place(chip_x, y, z, 1 - core), ps.at[((0 * 2 + 0) * depth + origin) * 2 + half])
+
+    def second(valid, origin, half):
+        if half == 0:
+            unit = number(chip_x, 1 - y, origin, core)
+        else:
+            unit = number(1 - chip_x, y, origin, core)
+        arrive(valid, unit, half)
+        source = xall.at[half, unit]
+        if half == 0:
+            send(valid, source, unit, half, place(1 - chip_x, y, z, core), xs.at[2 * depth + origin])
+        else:
+            send(valid, source, unit, half, place(chip_x, 1 - y, z, core), ys.at[2 * depth + origin])
+        send(valid, source, unit, half, place(chip_x, y, z, 1 - core), ps.at[((0 * 2 + 1) * depth + origin) * 2 + half])
+
+    def third(valid, origin, half):
+        near = number(1 - chip_x, y, origin, core) if half == 0 else number(chip_x, 1 - y, origin, core)
+        far = number(1 - chip_x, 1 - y, origin, core)
+        for row, unit in enumerate((near, far)):
+            arrive(valid, unit, half)
+            send(valid, xall.at[half, unit], unit, half, place(chip_x, y, z, 1 - core), ps.at[((1 * 2 + row) * depth + origin) * 2 + half])
+
+    always = z >= 0
+    own = pltpu.make_async_copy(m_ref.at[me], rall.at[me], local.at[2])
+    own.start()
+    keeps = []
+    for half in range(2):
+        keep = pltpu.make_async_copy(x_ref.at[:, pl.ds(half * cols, cols)], xall.at[half, me], local.at[half])
+        keep.start()
+        keeps.append(keep)
+        along_z(always, True, 0, half)
+        along_z(always, False, 0, half)
+    for half in range(2):
+        spread(always, z, 0, half)
+
+    def messages(part):
+        for i, other in enumerate(others):
+            if i % 3 != part:
+                continue
+            there = other[0] * shards + other[1]
+            copy = pltpu.make_async_remote_copy(
+                src_ref=m_ref.at[there],
+                dst_ref=rall.at[me],
+                send_sem=gs.at[i],
+                recv_sem=gr.at[me],
+                device_id=other,
+                device_id_type=MESH,
+            )
+            copy.start()
+            pending.append((always, copy))
+
+    for k in range(depth + 2):
+        if 1 <= k < depth:
+            for half in range(2):
+                for up in (True, False):
+                    origin = z - k if up else z + k
+                    valid = z >= k if up else z + k <= depth - 1
+                    arrive(valid, number(chip_x, y, origin, core), half)
+                    along_z(valid, up, k, half)
+            for half in range(2):
+                for up in (True, False):
+                    origin = z - k if up else z + k
+                    valid = z >= k if up else z + k <= depth - 1
+                    spread(valid, origin, k, half)
+            messages(k - 1)
+        if 1 <= k <= depth:
+            j = k - 1
+            for half in range(2):
+                if j == 0:
+                    second(always, z, half)
+                else:
+                    second(z >= j, z - j, half)
+                    second(z + j <= depth - 1, z + j, half)
+        if k >= 2:
+            j = k - 2
+            for half in range(2):
+                if j == 0:
+                    third(always, z, half)
+                else:
+                    third(z >= j, z - j, half)
+                    third(z + j <= depth - 1, z + j, half)
+    for px in range(2):
+        for py in range(pair):
+            for pz in range(depth):
+                for half in range(2):
+                    arrive(always, number(px, py, pz, 1 - core), half)
+    for other in others:
+        there = other[0] * shards + other[1]
+        pltpu.make_async_remote_copy(
+            src_ref=m_ref.at[there],
+            dst_ref=rall.at[there],
+            send_sem=gs.at[0],
+            recv_sem=gr.at[there],
+            device_id=(expert, shard),
+            device_id_type=MESH,
+        ).wait_recv()
+    for valid, copy in pending:
+        pl.when(valid)(copy.wait_send)
+    own.wait()
+    for keep in keeps:
+        keep.wait()
+
+
+def exchange(tokens, messages, group, shards):
+    total = group * shards
+    rows, width = tokens.shape
+    pair = group // 2
+    depth = shards // pair
+    dma = pltpu.SemaphoreType.DMA
+    anywhere = pl.BlockSpec(memory_space=pl.ANY)
+    return pl.pallas_call(
+        functools.partial(comm_kernel, group, shards, pair),
+        out_shape=(
+            jax.ShapeDtypeStruct((2, total, rows, width // 2), tokens.dtype),
+            jax.ShapeDtypeStruct(messages.shape, messages.dtype),
+        ),
+        in_specs=[pl.BlockSpec(memory_space=pltpu.VMEM), pl.BlockSpec(memory_space=pltpu.VMEM)],
+        out_specs=(anywhere, anywhere),
+        scratch_shapes=[
+            dma((4 * depth,)),
+            dma((3 * depth,)),
+            dma((3 * depth,)),
+            dma((8 * depth,)),
+            dma((total,)),
+            dma((2 * total,)),
+            dma((total,)),
+            dma((3,)),
+        ],
+        compiler_params=pltpu.CompilerParams(collective_id=0, has_side_effects=True),
+    )(tokens, messages)
+
+
+def leaf_inverse(work, unroll):
+    packs, size, lanes = work.shape
+    lane = lax.broadcasted_iota(jnp.int32, (8, lanes), 1)
+    inner = lax.rem(lane, size)
+    base = lane - inner
+
+    def step(i, carry):
+        j = i * 2
+        at0, at1 = inner == j, inner == j + 1
+        index0, index1 = base + j, base + j + 1
+        pivot = jnp.logical_or(at0, at1)
+        take = lambda v, ix: jnp.take_along_axis(v, ix, axis=1)
+        news = []
+        for p in range(packs):
+            r0 = jnp.broadcast_to(work[p, pl.ds(j, 1), :], (8, lanes))
+            r1 = jnp.broadcast_to(work[p, pl.ds(j + 1, 1), :], (8, lanes))
+            a, b = take(r0, index0), take(r0, index1)
+            c, d = take(r1, index0), take(r1, index1)
+            scale = 1.0 / (a * d - b * c)
+            r0 = jnp.where(at0, 1.0, jnp.where(at1, 0.0, r0))
+            r1 = jnp.where(at1, 1.0, jnp.where(at0, 0.0, r1))
+            news.append(((d * scale) * r0 - (b * scale) * r1, (a * scale) * r1 - (c * scale) * r0))
+        for p in range(packs):
+            s0, s1 = news[p]
+            for t in range(size // 8):
+                m = work[p, t * 8:(t + 1) * 8, :]
+                c0, c1 = take(m, index0), take(m, index1)
+                work[p, t * 8:(t + 1) * 8, :] = jnp.where(pivot, 0.0, m) - c0 * s0 - c1 * s1
+        for p in range(packs):
+            s0, s1 = news[p]
+            work[p, pl.ds(j, 1), :] = s0[:1]
+            work[p, pl.ds(j + 1, 1), :] = s1[:1]
+        return carry
+
+    lax.fori_loop(0, size // 2, step, 0, unroll=unroll)
+
+def invert(cov, work, side_ref, mid_ref, low_ref, leaf=64, unroll=False):
+    count, full, _ = cov.shape
+    per = 128 // leaf
+
+    def solve_leaf(offset):
+        for p in range(count // per):
+            parts = [cov[p * per + i, offset:offset + leaf, offset:offset + leaf] for i in range(per)]
+            work[p] = jnp.concatenate(parts, axis=1) if per > 1 else parts[0]
+        leaf_inverse(work, unroll)
+        for p in range(count // per):
+            for i in range(per):
+                cov[p * per + i, offset:offset + leaf, offset:offset + leaf] = work[p][:, i * leaf:(i + 1) * leaf]
+
+    def solve(offset, size):
+        if size == leaf:
+            solve_leaf(offset)
+            return
+        half = size // 2
+        one, two = slice(offset, offset + half), slice(offset + half, offset + size)
+        solve(offset, half)
+        store = side_ref if size == full else mid_ref if size == full // 2 else low_ref
+        for n in range(count):
+            upper = cov[n, one, two]
+            side = dot_f32(cov[n, one, one], upper)
+            store[n] = side
+            cov[n, two, two] = cov[n, two, two] - dot_f32(upper, side, TN)
+        solve(offset + half, half)
+        for n in range(count):
+            last = cov[n, two, two]
+            side = store[n]
+            corner = dot_f32(side, last)
+            cov[n, one, one] = cov[n, one, one] + dot_f32(corner, side, NT)
+            cov[n, one, two] = -corner
+            cov[n, two, one] = -corner.T
+    solve(0, full)
+
+
+def same(shape, rows, columns):
+    return rows(lax.broadcasted_iota(jnp.int32, shape, 0)) == columns(lax.broadcasted_iota(jnp.int32, shape, 1))
+
+
+def one_hot(mask):
+    return jnp.where(mask, 1.0, 0.0).astype(jnp.bfloat16)
+
+
+def inverse_kernel(
+    main, tokens, damp_a, damp_f, x_ref, m_ref, xc_ref, gc_ref, ahi_ref, alo_ref, shi_ref, slo_ref, cov, work, side, mid, low
+):
+    sources = m_ref.shape[0]
+    ff = gc_ref.shape[1]
+    blocks = ff // BLK
+    extra = main // blocks
+    batch = BLK // tokens
+    groups = sources // batch
+    rows_main, rows_extra = batch * main, batch * extra
+    rows_all = rows_main + rows_extra
+    width = x_ref.shape[2]
+    tile_main = one_hot(same((MARK, BLK), lambda i: i, lambda j: lax.rem(j, tokens)))
+    tile_extra = one_hot(same((MARK, BLK), lambda i: i - tokens, lambda j: lax.rem(j, tokens)))
+    owner = same((rows_main, BLK), lambda i: i // main, lambda j: j // tokens)
+    first = one_hot(same((rows_extra, rows_main), lambda i: (i // extra) * main + lax.rem(i, extra), lambda j: j))
+    total = jnp.zeros((), jnp.float32)
+    for g in range(groups):
+        part = m_ref[g * batch : (g + 1) * batch].reshape(rows_main, -1)
+        marks = part[:, ff + BLK :]
+        pick = jnp.where(owner, dot_bf16(marks, tile_main), 0.0)
+        rest = jnp.where(owner, dot_bf16(marks, tile_extra), 0.0).astype(jnp.bfloat16)
+        rest = dot_bf16(first, rest)
+        total = total + jnp.sum(pick) + jnp.sum(rest)
+        pick, rest = pick.astype(jnp.bfloat16), rest.astype(jnp.bfloat16)
+        base = g * rows_all
+        for h in range(2):
+            rows = x_ref[h, g * BLK : (g + 1) * BLK, :]
+            xc_ref[base : base + rows_main, h * width : (h + 1) * width] = dot_bf16(pick, rows).astype(jnp.bfloat16)
+            xc_ref[base + rows_main : base + rows_all, h * width : (h + 1) * width] = dot_bf16(rest, rows).astype(
+                jnp.bfloat16
+            )
+        gc_ref[base : base + rows_main, :] = part[:, :ff]
+        for q in range(blocks):
+            chosen = one_hot(
+                same((rows_extra, rows_main), lambda i: (i // extra) * main + q * extra + lax.rem(i, extra), lambda j: j)
+            )
+            gc_ref[base + rows_main : base + rows_all, q * BLK : (q + 1) * BLK] = dot_bf16(
+                chosen, part[:, ff : ff + BLK]
+            ).astype(jnp.bfloat16)
+    scale = 1.0 / jnp.broadcast_to(total, (1, 1))
+    eye = same((BLK, BLK), lambda i: i, lambda j: j)
+    count_a = ahi_ref.shape[0]
+    for b in range(count_a):
+        rows = xc_ref[:, b * BLK : (b + 1) * BLK]
+        cov[b] = dot_bf16(rows, rows, TN) * scale + jnp.where(eye, damp_a[b], 0.0)
+    for b in range(blocks):
+        rows = gc_ref[:, b * BLK : (b + 1) * BLK]
+        cov[count_a + b] = dot_bf16(rows, rows, TN) * scale + jnp.where(eye, damp_f[b], 0.0)
+    invert(cov, work, side, mid, low)
+    for b in range(count_a):
+        ahi_ref[b], alo_ref[b] = split(cov[b], 2)
+    for b in range(blocks):
+        shi_ref[b], slo_ref[b] = split(cov[count_a + b], 2)
+
+
+def three(a, b, dims=NN):
+    return dot_bf16(a[0], b[1], dims) + dot_bf16(a[1], b[0], dims) + dot_bf16(a[0], b[0], dims)
+
+
+def precond_kernel(x_ref, g_ref, ahi_ref, alo_ref, shi_ref, slo_ref, out_ref, norm_ref):
+    gradient = dot_bf16(x_ref[...], g_ref[...], TN)
+    left = (ahi_ref[0], alo_ref[0])
+
+    @pl.when(pl.program_id(0) == 0)
+    def _():
+        norm_ref[...] = jnp.zeros_like(norm_ref)
+
+    for c in range(shi_ref.shape[0]):
+        columns = slice(c * BLK, (c + 1) * BLK)
+        right = three(split(gradient[:, columns], 2), (shi_ref[c], slo_ref[c]))
+        out = three(left, split(right, 2))
+        out_ref[:, columns] = out
+        norm_ref[:, columns] += jnp.sum((out * out).reshape(-1, 8, BLK), axis=0)
+
+
+def total_kernel(group, shards, scale, part_ref, out_ref, parts, send_sem, recv_sem):
+    expert = lax.axis_index("expert")
+    shard = lax.axis_index("shard")
+    me = expert * shards + shard
+    others = [
+        (lax.rem(expert + de, group), lax.rem(shard + ds, shards))
+        for ds in range(shards)
+        for de in range(group)
+        if de or ds
+    ]
+    barrier = pltpu.get_barrier_semaphore()
+    for other in others:
+        pl.semaphore_signal(barrier, 1, device_id=other, device_id_type=MESH)
+    pl.semaphore_wait(barrier, len(others))
+    copies = []
+    for i, other in enumerate(others):
+        copy = pltpu.make_async_remote_copy(
+            src_ref=part_ref,
+            dst_ref=parts.at[me],
+            send_sem=send_sem.at[i],
+            recv_sem=recv_sem.at[me],
+            device_id=other,
+            device_id_type=MESH,
+        )
+        copy.start()
+        copies.append(copy)
+    parts[me] = part_ref[...]
+    for other in others:
+        there = other[0] * shards + other[1]
+        pltpu.make_async_remote_copy(
+            src_ref=part_ref,
+            dst_ref=parts.at[there],
+            send_sem=send_sem.at[0],
+            recv_sem=recv_sem.at[there],
+            device_id=(expert, shard),
+            device_id_type=MESH,
+        ).wait_recv()
+    total = jnp.sum(jnp.sum(parts[...], axis=0))
+    out_ref[...] = lax.rsqrt(jnp.broadcast_to(total, out_ref.shape) * scale + 1e-06)
+    for copy in copies:
+        copy.wait_send()
+
+
+def total_scale(part, group, shards, entries):
+    total = group * shards
+    dma = pltpu.SemaphoreType.DMA
+    vmem = pl.BlockSpec(memory_space=pltpu.VMEM)
+    return pl.pallas_call(
+        functools.partial(total_kernel, group, shards, 1.0 / entries),
+        out_shape=jax.ShapeDtypeStruct((8, 128), jnp.float32),
+        in_specs=[vmem],
+        out_specs=vmem,
+        scratch_shapes=[pltpu.VMEM((total, 8, 128), jnp.float32), dma((total,)), dma((total,))],
+        compiler_params=pltpu.CompilerParams(collective_id=1, has_side_effects=True),
+    )(part)
+
+
+def capacity_of(tok_rows, group_count):
+    return min(tok_rows, max(2, 5 * tok_rows // (2 * group_count)))
+
+
+def fast(tokens_in, out_grad, expert_ids, d_levels, f_levels):
+    group_count = lax.axis_size("expert")
+    shard_count = lax.axis_size("shard")
+    tok_rows, width = tokens_in.shape
+    ff_full = out_grad.shape[2]
+    ff_dev = ff_full // shard_count
+    blocks = ff_dev // BLK
+    count_a = width // BLK
+    capacity = capacity_of(tok_rows, group_count)
+    main = 16 * (capacity // 16)
+    extra = capacity - main
+    total = group_count * shard_count
+    flat_ids = expert_ids.reshape(-1)
+    member = (flat_ids[:, None] == jnp.arange(group_count, dtype=jnp.int32)[None, :]).astype(jnp.int32)
+    before = jnp.cumsum(member, axis=0) - member
+    ranking = jnp.sum(before * member, axis=1)
+    target = flat_ids * capacity + ranking
+    dispatch = (jnp.arange(group_count * capacity, dtype=jnp.int32)[:, None] == target[None, :]).astype(jnp.bfloat16)
+    per_token = jnp.sum(dispatch.reshape(-1, tok_rows, 2).astype(jnp.float32), axis=2).astype(jnp.bfloat16)
+    sent = jnp.dot(dispatch, out_grad.reshape(2 * tok_rows, ff_full), preferred_element_type=jnp.float32)
+    sent = sent.astype(jnp.bfloat16).reshape(group_count, capacity, ff_full)
+    marks = per_token.reshape(group_count, capacity, tok_rows)
+    first = sent[:, :main].reshape(group_count, main, shard_count, ff_dev).transpose(0, 2, 1, 3)
+    last = sent[:, main:].reshape(group_count, extra, shard_count, blocks, BLK).transpose(0, 2, 3, 1, 4)
+    info = jnp.concatenate(
+        (
+            marks[:, :main],
+            jnp.pad(marks[:, main:], ((0, 0), (0, main - extra), (0, 0))),
+            jnp.zeros((group_count, main, MARK - 2 * tok_rows), jnp.bfloat16),
+        ),
+        axis=2,
+    )
+    messages = jnp.concatenate(
+        (
+            first.reshape(total, main, ff_dev),
+            last.reshape(total, main, BLK),
+            jnp.broadcast_to(info[:, None], (group_count, shard_count, main, MARK)).reshape(total, main, MARK),
+        ),
+        axis=2,
+    )
+    rows_x, rows_m = exchange(tokens_in, messages, group_count, shard_count)
+    rows_x = rows_x.reshape(2, total * tok_rows, width // 2)
+
+    row_total = total * capacity
+    count = count_a + blocks
+    vmem = pl.BlockSpec(memory_space=pltpu.VMEM)
+    smem = pl.BlockSpec(memory_space=pltpu.SMEM)
+    f32 = jnp.float32
+    xc, gc, ahi, alo, shi, slo = pl.pallas_call(
+        functools.partial(inverse_kernel, main, tok_rows),
+        out_shape=(
+            jax.ShapeDtypeStruct((row_total, width), jnp.bfloat16),
+            jax.ShapeDtypeStruct((row_total, ff_dev), jnp.bfloat16),
+            jax.ShapeDtypeStruct((count_a, BLK, BLK), jnp.bfloat16),
+            jax.ShapeDtypeStruct((count_a, BLK, BLK), jnp.bfloat16),
+            jax.ShapeDtypeStruct((blocks, BLK, BLK), jnp.bfloat16),
+            jax.ShapeDtypeStruct((blocks, BLK, BLK), jnp.bfloat16),
+        ),
+        in_specs=[smem, smem, vmem, vmem],
+        out_specs=(vmem,) * 6,
+        scratch_shapes=[
+            pltpu.VMEM((count, BLK, BLK), f32),
+            pltpu.VMEM((count // 2, 64, 128), f32),
+            pltpu.VMEM((count, HALF, HALF), f32),
+            pltpu.VMEM((count, HALF // 2, HALF // 2), f32),
+            pltpu.VMEM((count, HALF // 4, HALF // 4), f32),
+        ],
+        compiler_params=pltpu.CompilerParams(vmem_limit_bytes=48 << 20),
+    )(damping(d_levels[0]), damping(f_levels[0]), rows_x, rows_m)
+
+    precond, squares = pl.pallas_call(
+        precond_kernel,
+        grid=(count_a,),
+        out_shape=(
+            jax.ShapeDtypeStruct((width, ff_dev), f32),
+            jax.ShapeDtypeStruct((8, ff_dev), f32),
+        ),
+        in_specs=[
+            pl.BlockSpec((row_total, BLK), lambda b: (0, b)),
+            pl.BlockSpec((row_total, ff_dev), lambda b: (0, 0)),
+            pl.BlockSpec((1, BLK, BLK), lambda b: (b, 0, 0)),
+            pl.BlockSpec((1, BLK, BLK), lambda b: (b, 0, 0)),
+            pl.BlockSpec((blocks, BLK, BLK), lambda b: (0, 0, 0)),
+            pl.BlockSpec((blocks, BLK, BLK), lambda b: (0, 0, 0)),
+        ],
+        out_specs=(
+            pl.BlockSpec((BLK, ff_dev), lambda b: (b, 0)),
+            pl.BlockSpec((8, ff_dev), lambda b: (0, 0)),
+        ),
+        compiler_params=pltpu.CompilerParams(dimension_semantics=("arbitrary",), vmem_limit_bytes=32 << 20),
+    )(xc, gc, ahi, alo, shi, slo)
+    part = jnp.sum(squares.reshape(8, -1, 128), axis=1)
+    scale = total_scale(part, group_count, shard_count, group_count * width * ff_full)
+    return (precond * scale[0, 0]).astype(jnp.bfloat16)[None]
+
+
+def local(tokens_in, out_grad, expert_ids, d_levels, f_levels):
+    group_count = lax.axis_size("expert")
+    shard_count = lax.axis_size("shard")
+    tok_rows, width = tokens_in.shape
+    blocks = out_grad.shape[2] // shard_count // BLK
+    main = 16 * (capacity_of(tok_rows, group_count) // 16)
+    extra = capacity_of(tok_rows, group_count) - main
+    chips = group_count // 2 == 2 and shard_count % 2 == 0
+    packed = main > 0 and extra * blocks == main and 2 * tok_rows <= MARK and BLK % tok_rows == 0
+    even = (group_count * shard_count * tok_rows) % BLK == 0 and (width // BLK + blocks) % 2 == 0
+    small = group_count * shard_count * tok_rows * width * 2 <= 12 << 20
+    if chips and packed and even and small:
+        return fast(tokens_in, out_grad, expert_ids, d_levels, f_levels)
+    return plain(tokens_in, out_grad, expert_ids, d_levels, f_levels)
+
+
 def solution(mesh):
     return jax.shard_map(
         local,

time: 371 us -> 199 us (0.54)
  waiting for transfers between devices: 164 us -> 0 us
  Pallas kernels: 124 us -> 172 us
  blocking collectives: 38.6 us -> 0 us
  between operations: 14.3 us -> 0.15 us
  starting transfers between devices: 7.41 us -> 0 us
    all_gather x2 -> x0, waiting for transfers between devices: 103 us -> none  [the longest x1 86.6 us: local(): rows_x = lax.all_gather(own_x, 'shard', axis=0)]
    all_to_all x1 -> x0, waiting for transfers between devices: 59.9 us -> none  [local(): lax.all_to_all(send, ('expert', 'shard'), split_axis=0, concat_axis=0, ti...]
    pallas_call x3 -> x4, Pallas kernels: 124 us -> 172 us  [the longest x1 65.8 us: fast(): pl.pallas_call(functools.partial(inverse_kernel, main, tok_rows), out_sha...]
    psum x1 -> x0, blocking collectives: 38.6 us -> none  [local(): norm_total = lax.psum(jnp.sum(squares), ('expert', 'shard'))]
    all_to_all x1 -> x0, starting transfers between devices: 7.32 us -> none  [local(): lax.all_to_all(send, ('expert', 'shard'), split_axis=0, concat_axis=0, ti...]
    unnamed x13 -> x9, local copies, waits for them, and re-layouts: 1.89 us -> 6.91 us
  transfers between devices with their start and end apart: 3 -> 0, of which waited for: 3 -> 0; matrix products, arithmetic and copies ran while one was open for 0% -> 0% of each run, Pallas kernels for 14% -> 0%
where the time goes in v1:
time: 199 us
  Pallas kernels  172 us (86%)
  other arithmetic  14.7 us (7%)
  local copies, waits for them, and re-layouts  11.5 us (6%)
    pallas_call x1, Pallas kernels, fast(): pl.pallas_call(functools.partial(inverse_kernel, main, tok_rows), out_sha...  65.8 us
    pallas_call x1, Pallas kernels, exchange(): pl.pallas_call(functools.partial(comm_kernel, group, shards, pair), out_s...  64 us
    pallas_call x1, Pallas kernels, fast(): pl.pallas_call(precond_kernel, grid=(count_a,), out_shape=(jax.ShapeDtype...  32.4 us
    broadcast_in_dim x1, other arithmetic, fast(): return (precond * scale[0, 0]).astype(jnp.bfloat16)[None]  10.3 us
    pallas_call x1, Pallas kernels, total_scale(): pl.pallas_call(functools.partial(total_kernel, group, shards, 1.0 / entri...  9.97 us
    unnamed x9, local copies, waits for them, and re-layouts  6.91 us

profile of v1, /device:TPU:0, one launch (start us, length us, event | category | flops | bytes accessed | tf_op | source)
XLA Modules:
  0.0 199.0 jit_solution(15629913682857797225)
XLA Ops:
  0.0 0.7 multiply_bitcast_fusion.1.damp_a
  0.7 0.7 multiply_bitcast_fusion.damp_f
  1.3 0.1 pad.10.clone
  1.4 0.8 copy.24
  2.2 0.1 reshape.65
  2.3 0.1 fusion.1
  2.4 0.1 reduce_window_sum.11
  2.5 0.2 select_reduce_fusion
  2.7 0.1 reduce_sum.33
  2.8 0.1 copy.27
  2.8 0.7 multiply_add_fusion
  3.5 0.1 fusion.8
  3.6 0.1 reshape.72
  3.7 0.1 copy.28
  3.8 0.1 slice.23
  3.9 0.1 copy.30
  4.0 0.1 fusion.7
  4.1 1.5 reshape.66
  5.6 0.5 convolution_convert_fusion
  6.1 0.4 reshape.67
  6.5 0.1 slice.21
  6.5 0.1 slice.20
  6.6 0.6 copy.31
  7.2 0.1 bitcast_bitcast_fusion
  7.3 0.6 copy.25
  7.9 0.1 reshape.71
  8.0 1.2 pad_maximum_fusion.m_ref
  9.2 64.0 %shard_map.55 = (bf16[2,32,32,2048]{3,2,1,0:T(8,128)(2,1)}, bf16[32,16,1408]{2,1,0:T(8,128)(2,1)}) custom-call(bf16[32,4096]{1,0:T(8,128)(2,1)} %x_ref.1, bf16[32,16,1408]{2,1,0:T(8,128)(2,1)} %pad_maximum_fusion.m_ref), custom_call_target="tpu_custom_call" | custom-call | tf_op jit(solution)/shard_map/pallas_call | solution.py:417
  73.2 0.0 copy-start.2
  73.2 1.4 copy-done.2
  74.6 65.8 %shard_map.56 = (bf16[640,4096]{1,0:T(8,128)(2,1)}, bf16[640,1024]{1,0:T(8,128)(2,1)S(1)}, bf16[16,256,256]{2,1,0:T(8,128)(2,1)S(1)}, bf16[16,256,256]{2,1,0:T(8...) custom-call(f32[16]{0:T(128)S(1)} %multiply_bitcast_fusion.1.damp_a, ...), custom_call_target="tpu_custom_call" | custom-call | tf_op jit(solution)/shard_map/pallas_call | solution.py:705
  140.4 0.0 copy-start
  140.4 2.5 %copy-done = bf16[640,4096]{1,0:T(8,128)(2,1)S(1)} copy-done((bf16[640,4096]{1,0:T(8,128)(2,1)S(1)}, bf16[640,4096]{1,0:T(8,128)(2,1)}, u32[]{:S(2)}) %copy-start) | copy-done | bytes 5242904
  142.9 0.0 copy-start.1
  142.9 1.6 copy-done.1
  144.5 32.4 %shard_map.57 = (f32[4096,1024]{1,0:T(8,128)}, f32[8,1024]{1,0:T(8,128)S(1)}) custom-call(bf16[640,4096]{1,0:T(8,128)(2,1)S(1)} %copy-done, bf16[640,1024]{1,0:T(8,128)(2,1)S(1)} %get-tuple-element.18.g_ref, bf16[16,256,256]{2,1,0:T(8,128)(2,1)S(1)} %get-tuple-element.19.ahi_ref, bf16[16,256,256]{2,1,0:T(8,128)(2,1)S(1)} %copy-done.1, ...), custom_call_target="tpu_custom_call" | custom-call | tf_op jit(solution)/shard_map/pallas_call | solution.py:727
  176.9 0.6 bitcast_reduce_fusion.part_ref
  177.5 10.0 %shard_map.58 = f32[8,128]{1,0:T(8,128)} custom-call(f32[8,128]{1,0:T(8,128)} %bitcast_reduce_fusion.part_ref), custom_call_target="tpu_custom_call" | custom-call | tf_op jit(solution)/shard_map/pallas_call | solution.py:643
  187.5 1.3 slice.19
  188.8 10.3 %fusion = bf16[1,4096,1024]{2,1,0:T(8,128)(2,1)} fusion(f32[4096,1024]{1,0:T(8,128)} %get-tuple-element.23, f32[]{:T(128)} %bitcast.9), kind=kLoop, calls=%fused_computation.2 | loop fusion | flops 8388608 | bytes 25165828 | tf_op jit(solution)/shard_map/broadcast_in_dim | solution.py:750
  (3 shorter events, 0.0 us)
Async XLA Ops:
  73.2 1.4 copy-start.2
  140.4 2.5 %copy-start = (bf16[640,4096]{1,0:T(8,128)(2,1)S(1)}, bf16[640,4096]{1,0:T(8,128)(2,1)}, u32[]{:S(2)}) copy-start(bf16[640,4096]{1,0:T(8,128)(2,1)} %get-tuple-element.17.x_ref) | copy-start | bytes 15728644
  142.9 1.6 copy-start.1

commit v2 on v0

--- a/solution.py
+++ b/solution.py
@@ -10,6 +10,9 @@
 BLK = 256
 HALF = BLK // 2
 MARK = 128
+LEAF = 64
+MESH = pl.DeviceIdType.MESH
+NN = (((1,), (0,)), ((), ()))
 NT = (((1,), (1,)), ((), ()))
 TN = (((0,), (0,)), ((), ()))
 
@@ -142,7 +145,7 @@
     )(damp, row_count, rows)
 
 
-def local(tokens_in, out_grad, expert_ids, d_levels, f_levels):
+def plain(tokens_in, out_grad, expert_ids, d_levels, f_levels):
     group_count = lax.axis_size("expert")
     shard_count = lax.axis_size("shard")
     tok_rows = tokens_in.shape[0]
@@ -237,6 +240,598 @@
     return (precond * ascent_scale).astype(jnp.bfloat16)[None]
 
 
+class Exchange:
+    def __init__(self, group, shards, x_ref, m_ref, xall, rall, sems):
+        self.group, self.shards = group, shards
+        self.x_ref, self.m_ref, self.xall, self.rall = x_ref, m_ref, xall, rall
+        self.zs, self.ys, self.xs, self.ps, self.gs, self.xr, self.gr, self.own = sems
+        self.expert = lax.axis_index("expert")
+        self.shard = lax.axis_index("shard")
+        self.pair = group // 2
+        self.depth = shards // self.pair
+        self.x, self.core = self.expert // 2, lax.rem(self.expert, 2)
+        self.z, self.y = self.shard // self.pair, lax.rem(self.shard, self.pair)
+        self.me = self.expert * shards + self.shard
+        self.always = self.z >= 0
+        self.pending = []
+        self.local = []
+        self.others = [
+            (lax.rem(self.expert + de, group), lax.rem(self.shard + ds, shards))
+            for ds in range(shards)
+            for de in range(group)
+            if de or ds
+        ]
+
+    def place(self, x, y, z, core):
+        return (x * 2 + core, z * self.pair + y)
+
+    def number(self, x, y, z, core):
+        return (x * 2 + core) * self.shards + z * self.pair + y
+
+    def barrier(self):
+        barrier = pltpu.get_barrier_semaphore()
+        for other in self.others:
+            pl.semaphore_signal(barrier, 1, device_id=other, device_id_type=MESH)
+        pl.semaphore_wait(barrier, len(self.others))
+
+    def source(self, k, part, unit):
+        columns = self.xall.shape[3]
+        if k == 0:
+            return self.x_ref.at[:, pl.ds(part * columns, columns)]
+        return self.xall.at[part, unit]
+
+    def send(self, valid, source, unit, part, target, sem):
+        copy = pltpu.make_async_remote_copy(
+            src_ref=source,
+            dst_ref=self.xall.at[part, unit],
+            send_sem=sem,
+            recv_sem=self.xr.at[unit * self.xall.shape[0] + part],
+            device_id=target,
+            device_id_type=MESH,
+        )
+        pl.when(valid)(copy.start)
+        self.pending.append((valid, copy))
+
+    def arrive(self, valid, unit, part):
+        @pl.when(valid)
+        def _():
+            pltpu.make_async_remote_copy(
+                src_ref=self.xall.at[part, unit],
+                dst_ref=self.xall.at[part, unit],
+                send_sem=self.zs.at[0],
+                recv_sem=self.xr.at[unit * self.xall.shape[0] + part],
+                device_id=(self.expert, self.shard),
+                device_id_type=MESH,
+            ).wait_recv()
+
+    def sides(self, k):
+        if k == 0:
+            return [(None, self.always, self.z)]
+        return [
+            (True, self.z >= k, self.z - k),
+            (False, self.z + k <= self.depth - 1, self.z + k),
+        ]
+
+    def along(self, k, part):
+        parts = self.xall.shape[0]
+        for side, valid, origin in self.sides(k):
+            unit = self.number(self.x, self.y, origin, self.core)
+            if k:
+                self.arrive(valid, unit, part)
+            for up in (True, False) if side is None else (side,):
+                more = jnp.logical_and(valid, self.z < self.depth - 1 if up else self.z > 0)
+                target = self.place(self.x, self.y, self.z + (1 if up else -1), self.core)
+                sem = self.zs.at[(k * parts + part) * 2 + int(up)]
+                self.send(more, self.source(k, part, unit), unit, part, target, sem)
+
+    def beside(self, valid, source, unit, part, axis, sem):
+        x, y = (1 - self.x, self.y) if axis == "x" else (self.x, 1 - self.y)
+        sems = self.xs if axis == "x" else self.ys
+        self.send(valid, source, unit, part, self.place(x, y, self.z, self.core), sems.at[sem])
+
+    def across(self, valid, source, unit, part, sem):
+        target = self.place(self.x, self.y, self.z, 1 - self.core)
+        self.send(valid, source, unit, part, target, self.ps.at[sem])
+
+    def spread(self, k, part):
+        parts = self.xall.shape[0]
+        for _, valid, origin in self.sides(k):
+            unit = self.number(self.x, self.y, origin, self.core)
+            source = self.source(k, part, unit)
+            for axis in ("y", "x") if part % 2 == 0 else ("x", "y"):
+                self.beside(valid, source, unit, part, axis, origin * parts + part)
+            self.across(valid, source, unit, part, origin * parts + part)
+
+    def second(self, k, part):
+        parts, depth = self.xall.shape[0], self.depth
+        for _, valid, origin in self.sides(k):
+            if part % 2 == 0:
+                unit, axis = self.number(self.x, 1 - self.y, origin, self.core), "x"
+            else:
+                unit, axis = self.number(1 - self.x, self.y, origin, self.core), "y"
+            self.arrive(valid, unit, part)
+            source = self.xall.at[part, unit]
+            self.beside(valid, source, unit, part, axis, (depth + origin) * parts + part)
+            self.across(valid, source, unit, part, (depth + origin) * parts + part)
+
+    def third(self, k, part):
+        parts, depth = self.xall.shape[0], self.depth
+        for _, valid, origin in self.sides(k):
+            if part % 2 == 0:
+                near = self.number(1 - self.x, self.y, origin, self.core)
+            else:
+                near = self.number(self.x, 1 - self.y, origin, self.core)
+            far = self.number(1 - self.x, 1 - self.y, origin, self.core)
+            for row, unit in enumerate((near, far)):
+                self.arrive(valid, unit, part)
+                sem = ((2 + row) * depth + origin) * parts + part
+                self.across(valid, self.xall.at[part, unit], unit, part, sem)
+
+    def begin(self, parts):
+        for part in parts:
+            self.along(0, part)
+        for part in parts:
+            self.spread(0, part)
+
+    def keep(self):
+        columns = self.xall.shape[3]
+        for part in range(self.xall.shape[0]):
+            source = self.x_ref.at[:, pl.ds(part * columns, columns)]
+            self.local.append(pltpu.make_async_copy(source, self.xall.at[part, self.me], self.own.at[part]))
+        self.local.append(
+            pltpu.make_async_copy(self.m_ref.at[self.me], self.rall.at[self.me], self.own.at[self.xall.shape[0]])
+        )
+        for copy in self.local:
+            copy.start()
+
+    def step(self, k, parts):
+        if k < self.depth:
+            for part in parts:
+                self.along(k, part)
+            for part in parts:
+                self.spread(k, part)
+        if k <= self.depth:
+            for part in parts:
+                self.second(k - 1, part)
+        if k >= 2:
+            for part in parts:
+                self.third(k - 2, part)
+
+    def finish(self, parts):
+        for x in range(2):
+            for y in range(self.pair):
+                for z in range(self.depth):
+                    for part in parts:
+                        self.arrive(self.always, self.number(x, y, z, 1 - self.core), part)
+
+    def messages(self, turn, turns):
+        for i, other in enumerate(self.others):
+            if i % turns != turn:
+                continue
+            copy = pltpu.make_async_remote_copy(
+                src_ref=self.m_ref.at[other[0] * self.shards + other[1]],
+                dst_ref=self.rall.at[self.me],
+                send_sem=self.gs.at[i],
+                recv_sem=self.gr.at[self.me],
+                device_id=other,
+                device_id_type=MESH,
+            )
+            copy.start()
+            self.pending.append((self.always, copy))
+
+    def wait_messages(self):
+        for other in self.others:
+            there = other[0] * self.shards + other[1]
+            pltpu.make_async_remote_copy(
+                src_ref=self.m_ref.at[there],
+                dst_ref=self.rall.at[there],
+                send_sem=self.gs.at[0],
+                recv_sem=self.gr.at[there],
+                device_id=(self.expert, self.shard),
+                device_id_type=MESH,
+            ).wait_recv()
+
+    def drain(self):
+        for valid, copy in self.pending:
+            pl.when(valid)(copy.wait_send)
+
+
+def leaf_inverse(work, packs, service):
+    _, size, lanes = work.shape
+    lane = lax.broadcasted_iota(jnp.int32, (8, lanes), 1)
+    inner = lax.rem(lane, size)
+    base = lane - inner
+
+    def take(value, index):
+        return jnp.take_along_axis(value, index, axis=1)
+
+    def step(i, carry):
+        j = i * 2
+        at0, at1 = inner == j, inner == j + 1
+        index0, index1 = base + j, base + j + 1
+        pivot = jnp.logical_or(at0, at1)
+        rows = []
+        for p in range(packs):
+            r0 = jnp.broadcast_to(work[p, pl.ds(j, 1), :], (8, lanes))
+            r1 = jnp.broadcast_to(work[p, pl.ds(j + 1, 1), :], (8, lanes))
+            a, b = take(r0, index0), take(r0, index1)
+            c, d = take(r1, index0), take(r1, index1)
+            scale = 1.0 / (a * d - b * c)
+            r0 = jnp.where(at0, 1.0, jnp.where(at1, 0.0, r0))
+            r1 = jnp.where(at1, 1.0, jnp.where(at0, 0.0, r1))
+            rows.append(((d * scale) * r0 - (b * scale) * r1, (a * scale) * r1 - (c * scale) * r0))
+        for p in range(packs):
+            s0, s1 = rows[p]
+            for t in range(0, size, 8):
+                m = work[p, t : t + 8, :]
+                c0, c1 = take(m, index0), take(m, index1)
+                work[p, t : t + 8, :] = jnp.where(pivot, 0.0, m) - c0 * s0 - c1 * s1
+        for p in range(packs):
+            s0, s1 = rows[p]
+            work[p, pl.ds(j, 1), :] = s0[:1]
+            work[p, pl.ds(j + 1, 1), :] = s1[:1]
+        return carry
+
+    lax.fori_loop(0, size // 4, step, 0)
+    service()
+    lax.fori_loop(size // 4, size // 2, step, 0)
+    service()
+
+
+def invert(cov, first, count, work, side_ref, mid_ref, service):
+    full = cov.shape[1]
+    leaf = work.shape[1]
+    per = work.shape[2] // leaf
+
+    def solve_leaf(offset):
+        span = slice(offset, offset + leaf)
+        for p in range(count // per):
+            parts = [cov[first + p * per + i, span, span] for i in range(per)]
+            work[p] = jnp.concatenate(parts, axis=1)
+        leaf_inverse(work, count // per, service)
+        for p in range(count // per):
+            for i in range(per):
+                cov[first + p * per + i, span, span] = work[p][:, i * leaf : (i + 1) * leaf]
+
+    def solve(offset, size):
+        if size == leaf:
+            solve_leaf(offset)
+            return
+        half = size // 2
+        one, two = slice(offset, offset + half), slice(offset + half, offset + size)
+        solve(offset, half)
+        store = side_ref if size == full else mid_ref
+        for n in range(count):
+            m = first + n
+            upper = cov[m, one, two]
+            side = dot_f32(cov[m, one, one], upper)
+            store[n] = side
+            cov[m, two, two] = cov[m, two, two] - dot_f32(upper, side, TN)
+        solve(offset + half, half)
+        for n in range(count):
+            m = first + n
+            last = cov[m, two, two]
+            side = store[n]
+            corner = dot_f32(side, last)
+            cov[m, one, one] = cov[m, one, one] + dot_f32(corner, side, NT)
+            cov[m, one, two] = -corner
+            cov[m, two, one] = -corner.T
+
+    solve(0, full)
+
+
+def same(shape, rows, columns):
+    return rows(lax.broadcasted_iota(jnp.int32, shape, 0)) == columns(lax.broadcasted_iota(jnp.int32, shape, 1))
+
+
+def one_hot(mask):
+    return jnp.where(mask, 1.0, 0.0).astype(jnp.bfloat16)
+
+
+def three(a, b):
+    return dot_bf16(a[0], b[1]) + dot_bf16(a[1], b[0]) + dot_bf16(a[0], b[0])
+
+
+def fused_kernel(
+    group,
+    shards,
+    tokens,
+    main,
+    entries,
+    damp_a,
+    damp_f,
+    x_ref,
+    m_ref,
+    out_ref,
+    scale_ref,
+    xall,
+    rall,
+    picks,
+    xc,
+    gc,
+    cov,
+    work,
+    side,
+    mid,
+    norm,
+    parts,
+    *sems,
+):
+    part_send, part_recv = sems[-2:]
+    exchange = Exchange(group, shards, x_ref, m_ref, xall, rall, sems[:-2])
+    depth = exchange.depth
+    exchange.barrier()
+    exchange.begin((0, 1))
+    exchange.keep()
+    for k in range(1, depth + 2):
+        exchange.step(k, (0, 1))
+        if k <= 3:
+            exchange.messages(k - 1, 3)
+    exchange.begin((2, 3))
+    exchange.finish((0, 1))
+    exchange.wait_messages()
+    for copy in exchange.local:
+        copy.wait()
+
+    steps = list(range(1, depth + 2))
+
+    def service():
+        if steps:
+            exchange.step(steps.pop(0), (2, 3))
+
+    sources = group * shards
+    ff = gc.shape[1]
+    blocks = ff // BLK
+    extra = main // blocks
+    batch = BLK // tokens
+    groups = sources // batch
+    rows_main, rows_extra = batch * main, batch * extra
+    rows_all = rows_main + rows_extra
+    columns = xall.shape[3]
+    tile_main = one_hot(same((MARK, BLK), lambda i: i, lambda j: lax.rem(j, tokens)))
+    tile_extra = one_hot(same((MARK, BLK), lambda i: i - tokens, lambda j: lax.rem(j, tokens)))
+    owner = same((rows_main, BLK), lambda i: i // main, lambda j: j // tokens)
+
+    def chosen(shift):
+        mask = same((rows_extra, rows_main), lambda i: (i // extra) * main + shift + lax.rem(i, extra), lambda j: j)
+        return one_hot(mask)
+
+    total = jnp.zeros((), jnp.float32)
+    for g in range(groups):
+        part = rall[g * batch : (g + 1) * batch].reshape(rows_main, -1)
+        marks = part[:, ff + BLK :]
+        pick = jnp.where(owner, dot_bf16(marks, tile_main), 0.0)
+        rest = jnp.where(owner, dot_bf16(marks, tile_extra), 0.0).astype(jnp.bfloat16)
+        rest = dot_bf16(chosen(0), rest)
+        total = total + jnp.sum(pick) + jnp.sum(rest)
+        base = g * rows_all
+        picks[base : base + rows_main, :] = pick.astype(jnp.bfloat16)
+        picks[base + rows_main : base + rows_all, :] = rest.astype(jnp.bfloat16)
+        gc[base : base + rows_main, :] = part[:, :ff]
+        for q in range(blocks):
+            spread = dot_bf16(chosen(q * extra), part[:, ff : ff + BLK])
+            gc[base + rows_main : base + rows_all, q * BLK : (q + 1) * BLK] = spread.astype(jnp.bfloat16)
+
+    def select_rows(part):
+        for g in range(groups):
+            rows = xall[part, g * batch : (g + 1) * batch].reshape(BLK, columns)
+            span = slice(g * rows_all, (g + 1) * rows_all)
+            xc[span, part * columns : (part + 1) * columns] = dot_bf16(picks[span, :], rows).astype(jnp.bfloat16)
+
+    scale = 1.0 / jnp.broadcast_to(total, (1, 1))
+    eye = same((BLK, BLK), lambda i: i, lambda j: j)
+    count_a = xc.shape[1] // BLK
+    half = count_a // 2
+
+    def covariance(to, rows, damp):
+        cov[to] = dot_bf16(rows, rows, TN) * scale + jnp.where(eye, damp, 0.0)
+
+    def slot(b):
+        return b + jnp.where(b >= half, blocks, 0)
+
+    select_rows(0)
+    select_rows(1)
+    for b in range(half):
+        covariance(b, xc[:, b * BLK : (b + 1) * BLK], damp_a[b])
+    for b in range(blocks):
+        covariance(half + b, gc[:, b * BLK : (b + 1) * BLK], damp_f[b])
+    service()
+    invert(cov, 0, half + blocks, work, side, mid, service)
+    while steps:
+        service()
+    exchange.finish((2, 3))
+    select_rows(2)
+    select_rows(3)
+    for b in range(half, count_a):
+        covariance(blocks + b, xc[:, b * BLK : (b + 1) * BLK], damp_a[b])
+    invert(cov, half + blocks, half, work, side, mid, service)
+
+    norm[...] = jnp.zeros_like(norm)
+
+    def product(b, carry):
+        across = pl.multiple_of(b * BLK, BLK)
+        gradient = dot_bf16(xc[:, pl.ds(across, BLK)], gc[...], TN)
+        left = split(cov[slot(b)], 2)
+        for c in range(blocks):
+            right = three(split(gradient[:, c * BLK : (c + 1) * BLK], 2), split(cov[half + c], 2))
+            out = three(left, split(right, 2))
+            out_ref[pl.ds(across, BLK), c * BLK : (c + 1) * BLK] = out
+            norm[...] += jnp.sum((out * out).reshape(-1, 8, BLK), axis=0)
+        return carry
+
+    lax.fori_loop(0, count_a, product, 0)
+    parts[exchange.me] = norm[:, :MARK] + norm[:, MARK:]
+    exchange.drain()
+    copies = []
+    for i, other in enumerate(exchange.others):
+        copy = pltpu.make_async_remote_copy(
+            src_ref=parts.at[exchange.me],
+            dst_ref=parts.at[exchange.me],
+            send_sem=part_send.at[i],
+            recv_sem=part_recv.at[exchange.me],
+            device_id=other,
+            device_id_type=MESH,
+        )
+        copy.start()
+        copies.append(copy)
+    for other in exchange.others:
+        there = other[0] * shards + other[1]
+        pltpu.make_async_remote_copy(
+            src_ref=parts.at[there],
+            dst_ref=parts.at[there],
+            send_sem=part_send.at[0],
+            recv_sem=part_recv.at[there],
+            device_id=(exchange.expert, exchange.shard),
+            device_id_type=MESH,
+        ).wait_recv()
+    norm_total = jnp.sum(jnp.sum(parts[...], axis=0))
+    scale_ref[...] = lax.rsqrt(jnp.broadcast_to(norm_total, scale_ref.shape) * (1.0 / entries) + 1e-06)
+    for copy in copies:
+        copy.wait_send()
+
+
+def scale_kernel(value_ref, scale_ref, out_ref, slots, sems):
+    depth, rows = slots.shape[:2]
+    scale = scale_ref[0:1, 0:1]
+    count = value_ref.shape[0] // rows
+
+    def out(i):
+        to = pl.multiple_of(i * rows, rows)
+        at = lax.rem(i, depth)
+        return pltpu.make_async_copy(slots.at[at], out_ref.at[pl.ds(to, rows), :], sems.at[at])
+
+    def step(i, carry):
+        @pl.when(i >= depth)
+        def _():
+            out(i - depth).wait()
+
+        from_row = pl.multiple_of(i * rows, rows)
+        slots[lax.rem(i, depth)] = (value_ref[pl.ds(from_row, rows), :] * scale).astype(slots.dtype)
+        out(i).start()
+        return carry
+
+    lax.fori_loop(0, count, step, 0)
+    for i in range(count - depth, count):
+        out(i).wait()
+
+
+def capacity_of(tok_rows, group_count):
+    return min(tok_rows, max(2, 5 * tok_rows // (2 * group_count)))
+
+
+def pack_messages(out_grad, expert_ids, group_count, shard_count, capacity, main):
+    tok_rows, _, ff_full = out_grad.shape
+    ff_dev = ff_full // shard_count
+    extra = capacity - main
+    total = group_count * shard_count
+    flat_ids = expert_ids.reshape(-1)
+    member = (flat_ids[:, None] == jnp.arange(group_count, dtype=jnp.int32)[None, :]).astype(jnp.int32)
+    before = jnp.cumsum(member, axis=0) - member
+    ranking = jnp.sum(before * member, axis=1)
+    target = flat_ids * capacity + ranking
+    dispatch = (jnp.arange(group_count * capacity, dtype=jnp.int32)[:, None] == target[None, :]).astype(jnp.bfloat16)
+    per_token = jnp.sum(dispatch.reshape(-1, tok_rows, 2).astype(jnp.float32), axis=2).astype(jnp.bfloat16)
+    sent = jnp.dot(dispatch, out_grad.reshape(2 * tok_rows, ff_full), preferred_element_type=jnp.float32)
+    sent = sent.astype(jnp.bfloat16).reshape(group_count, capacity, ff_full)
+    marks = per_token.reshape(group_count, capacity, tok_rows)
+    first = sent[:, :main].reshape(group_count, main, shard_count, ff_dev).transpose(0, 2, 1, 3)
+    last = sent[:, main:].reshape(group_count, extra, shard_count, ff_dev // BLK, BLK).transpose(0, 2, 3, 1, 4)
+    info = jnp.concatenate(
+        (
+            marks[:, :main],
+            jnp.pad(marks[:, main:], ((0, 0), (0, main - extra), (0, 0))),
+            jnp.zeros((group_count, main, MARK - 2 * tok_rows), jnp.bfloat16),
+        ),
+        axis=2,
+    )
+    return jnp.concatenate(
+        (
+            first.reshape(total, main, ff_dev),
+            last.reshape(total, main, BLK),
+            jnp.broadcast_to(info[:, None], (group_count, shard_count, main, MARK)).reshape(total, main, MARK),
+        ),
+        axis=2,
+    )
+
+
+def fast(tokens_in, out_grad, expert_ids, d_levels, f_levels):
+    group_count = lax.axis_size("expert")
+    shard_count = lax.axis_size("shard")
+    tok_rows, width = tokens_in.shape
+    ff_full = out_grad.shape[2]
+    ff_dev = ff_full // shard_count
+    blocks = ff_dev // BLK
+    count_a = width // BLK
+    capacity = capacity_of(tok_rows, group_count)
+    main = 16 * (capacity // 16)
+    total = group_count * shard_count
+    depth = shard_count // (group_count // 2)
+    messages = pack_messages(out_grad, expert_ids, group_count, shard_count, capacity, main)
+    row_total = total * capacity
+    count = count_a // 2 + blocks
+    vmem = pl.BlockSpec(memory_space=pltpu.VMEM)
+    smem = pl.BlockSpec(memory_space=pltpu.SMEM)
+    f32, bf16, dma = jnp.float32, jnp.bfloat16, pltpu.SemaphoreType.DMA
+    precond, scale = pl.pallas_call(
+        functools.partial(fused_kernel, group_count, shard_count, tok_rows, main, group_count * width * ff_full),
+        out_shape=(
+            pltpu.VMEM((width, ff_dev), f32),
+            jax.ShapeDtypeStruct((8, 128), f32),
+        ),
+        in_specs=[smem, smem, vmem, vmem],
+        out_specs=(vmem, vmem),
+        scratch_shapes=[
+            pltpu.VMEM((4, total, tok_rows, width // 4), bf16),
+            pltpu.VMEM(messages.shape, bf16),
+            pltpu.VMEM((row_total, BLK), bf16),
+            pltpu.VMEM((row_total, width), bf16),
+            pltpu.VMEM((row_total, ff_dev), bf16),
+            pltpu.VMEM((count_a + blocks, BLK, BLK), f32),
+            pltpu.VMEM((count // 2, LEAF, 128), f32),
+            pltpu.VMEM((count, HALF, HALF), f32),
+            pltpu.VMEM((count, HALF // 2, HALF // 2), f32),
+            pltpu.VMEM((8, BLK), f32),
+            pltpu.VMEM((total, 8, MARK), f32),
+            dma((8 * depth,)),
+            dma((8 * depth,)),
+            dma((8 * depth,)),
+            dma((16 * depth,)),
+            dma((total,)),
+            dma((4 * total,)),
+            dma((total,)),
+            dma((5,)),
+            dma((total,)),
+            dma((total,)),
+        ],
+        compiler_params=pltpu.CompilerParams(collective_id=0, has_side_effects=True, vmem_limit_bytes=36 << 20),
+    )(damping(d_levels[0]), damping(f_levels[0]), tokens_in, messages)
+    ascent = pl.pallas_call(
+        scale_kernel,
+        out_shape=jax.ShapeDtypeStruct((width, ff_dev), bf16),
+        in_specs=[vmem, vmem],
+        out_specs=pl.BlockSpec(memory_space=pl.ANY),
+        scratch_shapes=[pltpu.VMEM((4, BLK, ff_dev), bf16), dma((4,))],
+        compiler_params=pltpu.CompilerParams(vmem_limit_bytes=8 << 20),
+    )(precond, scale)
+    return ascent[None]
+
+
+def local(tokens_in, out_grad, expert_ids, d_levels, f_levels):
+    group_count = lax.axis_size("expert")
+    shard_count = lax.axis_size("shard")
+    tok_rows, width = tokens_in.shape
+    blocks = out_grad.shape[2] // shard_count // BLK
+    main = 16 * (capacity_of(tok_rows, group_count) // 16)
+    extra = capacity_of(tok_rows, group_count) - main
+    chips = group_count // 2 == 2 and shard_count % 2 == 0
+    packed = main > 0 and extra * blocks == main and 2 * tok_rows <= MARK and BLK % tok_rows == 0
+    even = (group_count * shard_count * tok_rows) % BLK == 0 and width % (4 * BLK) == 0 and blocks % 2 == 0
+    small = group_count * shard_count * tok_rows * width * 2 <= 12 << 20
+    if chips and packed and even and small:
+        return fast(tokens_in, out_grad, expert_ids, d_levels, f_levels)
+    return plain(tokens_in, out_grad, expert_ids, d_levels, f_levels)
+
+
 def solution(mesh):
     return jax.shard_map(
         local,

time: 371 us -> 178 us (0.48)
  waiting for transfers between devices: 164 us -> 0 us
  Pallas kernels: 124 us -> 169 us
  blocking collectives: 38.6 us -> 0 us
  between operations: 14.3 us -> 0.32 us
  other arithmetic: 13.4 us -> 2.67 us
  starting transfers between devices: 7.41 us -> 0 us
  local copies, waits for them, and re-layouts: 9.13 us -> 4.97 us
    all_gather x2 -> x0, waiting for transfers between devices: 103 us -> none  [the longest x1 86.6 us: local(): rows_x = lax.all_gather(own_x, 'shard', axis=0)]
    all_to_all x1 -> x0, waiting for transfers between devices: 59.9 us -> none  [local(): lax.all_to_all(send, ('expert', 'shard'), split_axis=0, concat_axis=0, ti...]
    pallas_call x3 -> x2, Pallas kernels: 124 us -> 169 us  [the longest x1 165 us: fast(): pl.pallas_call(functools.partial(fused_kernel, group_count, shard_count,...]
    psum x1 -> x0, blocking collectives: 38.6 us -> none  [local(): norm_total = lax.psum(jnp.sum(squares), ('expert', 'shard'))]
    broadcast_in_dim x1 -> x0, other arithmetic: 9.6 us -> none  [local(): return (precond * ascent_scale).astype(jnp.bfloat16)[None]]
    all_to_all x1 -> x0, starting transfers between devices: 7.32 us -> none  [local(): lax.all_to_all(send, ('expert', 'shard'), split_axis=0, concat_axis=0, ti...]
  transfers between devices with their start and end apart: 3 -> 0, of which waited for: 3 -> 0; matrix products, arithmetic and copies ran while one was open for 0% -> 0% of each run, Pallas kernels for 14% -> 0%
where the time goes in v2:
time: 178 us; the launch traced here: 177 us
  Pallas kernels  169 us (95%)
  local copies, waits for them, and re-layouts  4.97 us (3%)
  other arithmetic  2.67 us (2%)
    pallas_call x1, Pallas kernels, fast(): pl.pallas_call(functools.partial(fused_kernel, group_count, shard_count,...  165 us
    pallas_call x1, Pallas kernels, fast(): pl.pallas_call(scale_kernel, out_shape=jax.ShapeDtypeStruct((width, ff_de...  4.21 us

profile of v2, /device:TPU:0, one launch (start us, length us, event | category | flops | bytes accessed | tf_op | source)
XLA Modules:
  0.0 177.4 jit_solution(3804646864125518812)
XLA Ops:
  0.0 0.7 multiply_bitcast_fusion.1.damp_a
  0.7 0.7 multiply_bitcast_fusion.damp_f
  1.3 0.1 pad.10.clone
  1.4 0.8 copy.24
  2.2 0.1 reshape.59
  2.3 0.1 fusion
  2.4 0.1 reduce_window_sum.11
  2.5 0.2 select_reduce_fusion
  2.7 0.1 reduce_sum.24
  2.8 0.1 copy.27
  2.8 0.7 multiply_add_fusion
  3.5 0.1 fusion.7
  3.6 0.1 reshape.66
  3.7 0.1 copy.28
  3.8 0.1 slice.19
  3.9 0.1 copy.30
  4.0 0.1 fusion.6
  4.1 1.5 reshape.60
  5.6 0.5 convolution_convert_fusion
  6.1 0.4 reshape.61
  6.5 0.1 slice.17
  6.5 0.1 slice.16
  6.6 0.6 copy.31
  7.2 0.1 bitcast_bitcast_fusion
  7.3 0.0 copy-start
  7.3 0.6 copy.25
  7.9 0.1 reshape.65
  8.0 0.1 pad_maximum_fusion.m_ref
  8.1 0.2 copy-done
  8.3 164.8 %shard_map.55 = (f32[4096,1024]{1,0:T(8,128)S(1)}, f32[8,128]{1,0:T(8,128)S(1)}) custom-call(f32[16]{0:T(128)S(1)} %multiply_bitcast_fusion.1.damp_a, f32[4]{0:T(128)S(1)} %multiply_bitcast_fusion.damp_f, bf16[32,4096]{1,0:T(8,128)(2,1)S(1)} %copy-done, bf16[32,16,1408]{2,1,0:T(8,128)(2,1)S(1)} %pad_maximum_fusion.m_ref), custom_call_target="tpu_custom_call" | custom-call | tf_op jit(solution)/shard_map/pallas_call | solution.py:775
  173.0 4.2 %shard_map.56 = bf16[4096,1024]{1,0:T(8,128)(2,1)} custom-call(f32[4096,1024]{1,0:T(8,128)S(1)} %get-tuple-element.7.value_ref, f32[8,128]{1,0:T(8,128)S(1)} %get-tuple-element.8.scale_ref), custom_call_target="tpu_custom_call" | custom-call | tf_op jit(solution)/shard_map/pallas_call | solution.py:808
  (3 shorter events, 0.0 us)
Async XLA Ops:
  7.3 1.0 copy-start

commit v3 on v2

--- a/solution.py
+++ b/solution.py
@@ -10,7 +10,7 @@
 BLK = 256
 HALF = BLK // 2
 MARK = 128
-LEAF = 64
+LEAF = 32
 MESH = pl.DeviceIdType.MESH
 NN = (((1,), (0,)), ((), ()))
 NT = (((1,), (1,)), ((), ()))
@@ -241,10 +241,11 @@
 
 
 class Exchange:
-    def __init__(self, group, shards, x_ref, m_ref, xall, rall, sems):
+    def __init__(self, group, shards, x_ref, m_ref, info_ref, xall, rall, iall, sems):
         self.group, self.shards = group, shards
-        self.x_ref, self.m_ref, self.xall, self.rall = x_ref, m_ref, xall, rall
-        self.zs, self.ys, self.xs, self.ps, self.gs, self.xr, self.gr, self.own = sems
+        self.x_ref, self.m_ref, self.info_ref = x_ref, m_ref, info_ref
+        self.xall, self.rall, self.iall = xall, rall, iall
+        self.zs, self.ys, self.xs, self.ps, self.gs, self.xr, self.gr, self.own, self.ns, self.nr = sems
         self.expert = lax.axis_index("expert")
         self.shard = lax.axis_index("shard")
         self.pair = group // 2
@@ -381,15 +382,48 @@
         self.local.append(
             pltpu.make_async_copy(self.m_ref.at[self.me], self.rall.at[self.me], self.own.at[self.xall.shape[0]])
         )
+        self.local.append(
+            pltpu.make_async_copy(
+                self.info_ref.at[self.expert], self.iall.at[self.me], self.own.at[self.xall.shape[0] + 1]
+            )
+        )
         for copy in self.local:
             copy.start()
 
+    def inform(self):
+        for i, other in enumerate(self.others):
+            copy = pltpu.make_async_remote_copy(
+                src_ref=self.info_ref.at[other[0]],
+                dst_ref=self.iall.at[self.me],
+                send_sem=self.ns.at[i],
+                recv_sem=self.nr.at[self.me],
+                device_id=other,
+                device_id_type=MESH,
+            )
+            copy.start()
+            self.pending.append((self.always, copy))
+
+    def wait_info(self):
+        for other in self.others:
+            there = other[0] * self.shards + other[1]
+            pltpu.make_async_remote_copy(
+                src_ref=self.iall.at[there],
+                dst_ref=self.iall.at[there],
+                send_sem=self.ns.at[0],
+                recv_sem=self.nr.at[there],
+                device_id=(self.expert, self.shard),
+                device_id_type=MESH,
+            ).wait_recv()
+
+    def relay(self, k, parts):
+        for part in parts:
+            self.along(k, part)
+        for part in parts:
+            self.spread(k, part)
+
     def step(self, k, parts):
         if k < self.depth:
-            for part in parts:
-                self.along(k, part)
-            for part in parts:
-                self.spread(k, part)
+            self.relay(k, parts)
         if k <= self.depth:
             for part in parts:
                 self.second(k - 1, part)
@@ -472,52 +506,111 @@
             work[p, pl.ds(j + 1, 1), :] = s1[:1]
         return carry
 
-    lax.fori_loop(0, size // 4, step, 0)
-    service()
-    lax.fori_loop(size // 4, size // 2, step, 0)
-    service()
-
-
-def invert(cov, first, count, work, side_ref, mid_ref, service):
+    lax.fori_loop(0, size // 2, step, 0)
+    if service is not None:
+        service()
+
+
+def invert(cov, first, count, work, tops, sides, quarter, side_ref, mid_ref, service):
     full = cov.shape[1]
-    leaf = work.shape[1]
-    per = work.shape[2] // leaf
-
-    def solve_leaf(offset):
-        span = slice(offset, offset + leaf)
-        for p in range(count // per):
-            parts = [cov[first + p * per + i, span, span] for i in range(per)]
-            work[p] = jnp.concatenate(parts, axis=1)
-        leaf_inverse(work, count // per, service)
-        for p in range(count // per):
-            for i in range(per):
-                cov[first + p * per + i, span, span] = work[p][:, i * leaf : (i + 1) * leaf]
-
-    def solve(offset, size):
-        if size == leaf:
-            solve_leaf(offset)
-            return
-        half = size // 2
-        one, two = slice(offset, offset + half), slice(offset + half, offset + size)
-        solve(offset, half)
-        store = side_ref if size == full else mid_ref
+    half = full // 2
+    leaf, lanes = work.shape[1:]
+    per = lanes // leaf
+    packs = count // per
+    diagonal = same((lanes, lanes), lambda i: i // leaf, lambda j: j // leaf)
+    group = lax.broadcasted_iota(jnp.int32, (leaf, lanes), 1) // leaf
+
+    def gather(p, rows, columns):
+        return jnp.concatenate([quarter[p * per + i, rows, columns] for i in range(per)], axis=1)
+
+    def scatter(p, rows, columns, value):
+        for i in range(per):
+            quarter[p * per + i, rows, columns] = value[:, i * leaf : (i + 1) * leaf]
+
+    def spread(value):
+        return jnp.where(diagonal, jnp.concatenate([value] * per, axis=0), 0.0)
+
+    def fold(value):
+        out = jnp.where(group == 0, value[:leaf], 0.0)
+        for i in range(1, per):
+            out = jnp.where(group == i, value[i * leaf : (i + 1) * leaf], out)
+        return out
+
+    def solve_pair(offset):
+        one, two = slice(offset, offset + leaf), slice(offset + leaf, offset + 2 * leaf)
+        for p in range(packs):
+            work[p] = gather(p, one, one)
+        leaf_inverse(work, packs, service)
+        for p in range(packs):
+            top = work[p]
+            upper = gather(p, one, two)
+            side = dot_f32(top, spread(upper))
+            tops[p] = top
+            sides[p] = side
+            work[p] = gather(p, two, two) - fold(dot_f32(upper, side, TN))
+        leaf_inverse(work, packs, service)
+        for p in range(packs):
+            last = work[p]
+            side = sides[p]
+            wide = spread(side)
+            corner = dot_f32(side, spread(last))
+            scatter(p, one, one, tops[p] + dot_f32(corner, wide, NT))
+            scatter(p, one, two, -corner)
+            scatter(p, two, one, -dot_f32(last, wide, NT))
+            scatter(p, two, two, last)
+
+    def solve_quarter():
+        one, two = slice(0, half // 2), slice(half // 2, half)
+        solve_pair(0)
+        for n in range(count):
+            upper = quarter[n, one, two]
+            side = dot_f32(quarter[n, one, one], upper)
+            mid_ref[n] = side
+            quarter[n, two, two] = quarter[n, two, two] - dot_f32(upper, side, TN)
+        solve_pair(half // 2)
+        for n in range(count):
+            last = quarter[n, two, two]
+            side = mid_ref[n]
+            corner = dot_f32(side, last)
+            quarter[n, one, one] = quarter[n, one, one] + dot_f32(corner, side, NT)
+            quarter[n, one, two] = -corner
+            quarter[n, two, one] = -corner.T
+
+    one, two = slice(0, half), slice(half, full)
+
+    def between():
         for n in range(count):
             m = first + n
             upper = cov[m, one, two]
-            side = dot_f32(cov[m, one, one], upper)
-            store[n] = side
-            cov[m, two, two] = cov[m, two, two] - dot_f32(upper, side, TN)
-        solve(offset + half, half)
-        for n in range(count):
-            m = first + n
-            last = cov[m, two, two]
-            side = store[n]
-            corner = dot_f32(side, last)
-            cov[m, one, one] = cov[m, one, one] + dot_f32(corner, side, NT)
-            cov[m, one, two] = -corner
-            cov[m, two, one] = -corner.T
-
-    solve(0, full)
+            top = quarter[n]
+            side = dot_f32(top, upper)
+            cov[m, one, one] = top
+            side_ref[n] = side
+            quarter[n] = cov[m, two, two] - dot_f32(upper, side, TN)
+
+    for n in range(count):
+        quarter[n] = cov[first + n, one, one]
+    if service is None:
+
+        def turn(h, carry):
+            solve_quarter()
+            pl.when(h == 0)(between)
+            return carry
+
+        lax.fori_loop(0, 2, turn, 0)
+    else:
+        solve_quarter()
+        between()
+        solve_quarter()
+    for n in range(count):
+        m = first + n
+        last = quarter[n]
+        side = side_ref[n]
+        corner = dot_f32(side, last)
+        cov[m, one, one] = cov[m, one, one] + dot_f32(corner, side, NT)
+        cov[m, one, two] = -corner
+        cov[m, two, one] = -corner.T
+        cov[m, two, two] = last
 
 
 def same(shape, rows, columns):
@@ -530,6 +623,57 @@
 
 def three(a, b):
     return dot_bf16(a[0], b[1]) + dot_bf16(a[1], b[0]) + dot_bf16(a[0], b[0])
+
+
+def pack_rows(group, shards, main, extra, tokens, ids_ref, g_ref, m_ref, info_ref):
+    slots = main + extra
+    pairs = ids_ref.shape[1]
+    ff = m_ref.shape[2] - BLK
+    blocks = ff // BLK
+    tall = info_ref.shape[1]
+    cut = MARK // tokens
+    ids = jnp.broadcast_to(ids_ref[...], (8, pairs))
+    expert = lax.broadcasted_iota(jnp.int32, (8, pairs), 0)
+    member = ids == expert
+    earlier = one_hot(lax.broadcasted_iota(jnp.int32, (pairs, pairs), 0) < lax.broadcasted_iota(jnp.int32, (pairs, pairs), 1))
+    rank = dot_bf16(one_hot(member), earlier)
+    rank = jnp.sum(jnp.where(member, rank, 0.0), axis=0, keepdims=True)
+    target = ids_ref[...] * slots + rank.astype(jnp.int32)
+
+    def matches(rows, wanted):
+        return wanted(lax.broadcasted_iota(jnp.int32, (rows, pairs), 0)) == target
+
+    pick = one_hot(matches(group * main, lambda i: (i // main) * slots + lax.rem(i, main)))
+    rest = matches(group * main, lambda i: (i // main) * slots + main + lax.rem(i, extra))
+    turn = lax.broadcasted_iota(jnp.int32, (group * main, pairs), 0) // extra
+    rest = jnp.concatenate(
+        [one_hot(jnp.logical_and(rest, lax.rem(turn, blocks) == q)) for q in range(blocks)], axis=1
+    )
+    for s in range(shards):
+        rows = g_ref[:, s * ff : (s + 1) * ff]
+        first = dot_bf16(pick, rows).astype(jnp.bfloat16)
+        tallest = jnp.concatenate([rows[:, q * BLK : (q + 1) * BLK] for q in range(blocks)], axis=0)
+        last = dot_bf16(rest, tallest).astype(jnp.bfloat16)
+        for e in range(group):
+            m_ref[e * shards + s, :, :ff] = first[e * main : (e + 1) * main]
+            m_ref[e * shards + s, :, ff:] = last[e * main : (e + 1) * main]
+    every = one_hot(matches(group * slots, lambda i: i))
+    own = one_hot(same((pairs, MARK), lambda i: i // 2, lambda j: lax.rem(j, tokens)))
+    marks = jnp.where(
+        same((group * slots, MARK), lambda i: lax.rem(lax.rem(i, slots), cut), lambda j: j // tokens),
+        dot_bf16(every, own),
+        0.0,
+    ).astype(jnp.bfloat16)
+    lift = one_hot(
+        same(
+            (group * tall, group * slots),
+            lambda i: i,
+            lambda j: (j // slots) * tall + lax.rem(j, slots) // cut,
+        )
+    )
+    info = dot_bf16(lift, marks).astype(jnp.bfloat16)
+    for e in range(group):
+        info_ref[e] = info[e * tall : (e + 1) * tall]
 
 
 def fused_kernel(
@@ -538,19 +682,26 @@
     tokens,
     main,
     entries,
-    damp_a,
-    damp_f,
+    level_a,
+    level_f,
     x_ref,
-    m_ref,
+    g_ref,
+    ids_ref,
     out_ref,
     scale_ref,
+    m_ref,
+    info_ref,
     xall,
     rall,
+    iall,
     picks,
     xc,
     gc,
     cov,
     work,
+    tops,
+    sides,
+    quarter,
     side,
     mid,
     norm,
@@ -558,59 +709,66 @@
     *sems,
 ):
     part_send, part_recv = sems[-2:]
-    exchange = Exchange(group, shards, x_ref, m_ref, xall, rall, sems[:-2])
+    exchange = Exchange(group, shards, x_ref, m_ref, info_ref, xall, rall, iall, sems[:-2])
     depth = exchange.depth
-    exchange.barrier()
-    exchange.begin((0, 1))
-    exchange.keep()
-    for k in range(1, depth + 2):
-        exchange.step(k, (0, 1))
-        if k <= 3:
-            exchange.messages(k - 1, 3)
-    exchange.begin((2, 3))
-    exchange.finish((0, 1))
-    exchange.wait_messages()
-    for copy in exchange.local:
-        copy.wait()
-
-    steps = list(range(1, depth + 2))
-
-    def service():
-        if steps:
-            exchange.step(steps.pop(0), (2, 3))
-
+    turns = 4
     sources = group * shards
     ff = gc.shape[1]
     blocks = ff // BLK
     extra = main // blocks
+    exchange.barrier()
+    exchange.begin((0, 1))
+    pack_rows(group, shards, main, extra, tokens, ids_ref, g_ref, m_ref, info_ref)
+    for k in range(1, depth + 2):
+        exchange.step(k, (0, 1))
+        if k == 1:
+            exchange.inform()
+            exchange.keep()
+        if k == depth - 1:
+            exchange.begin((2, 3))
+        if k == depth:
+            exchange.messages(0, turns)
+    exchange.wait_info()
+    for copy in exchange.local:
+        copy.wait()
+
+    late = (2, 3)
+    steps = []
+    for k in range(1, max(depth, turns)):
+        if k < depth:
+            steps.append(functools.partial(exchange.relay, k, late))
+        if k < turns:
+            steps.append(functools.partial(exchange.messages, k, turns))
+
+    def service():
+        if steps:
+            steps.pop(0)()
+
     batch = BLK // tokens
     groups = sources // batch
     rows_main, rows_extra = batch * main, batch * extra
     rows_all = rows_main + rows_extra
     columns = xall.shape[3]
-    tile_main = one_hot(same((MARK, BLK), lambda i: i, lambda j: lax.rem(j, tokens)))
-    tile_extra = one_hot(same((MARK, BLK), lambda i: i - tokens, lambda j: lax.rem(j, tokens)))
-    owner = same((rows_main, BLK), lambda i: i // main, lambda j: j // tokens)
-
-    def chosen(shift):
-        mask = same((rows_extra, rows_main), lambda i: (i // extra) * main + shift + lax.rem(i, extra), lambda j: j)
-        return one_hot(mask)
-
+    tall = iall.shape[1]
+    cut = MARK // tokens
+
+    def source_of(i):
+        return jnp.where(i < rows_main, i // main, (i - rows_main) // extra)
+
+    def slot_of(i):
+        return jnp.where(i < rows_main, lax.rem(i, main), main + lax.rem(i - rows_main, extra))
+
+    rise = one_hot(same((rows_all, batch * tall), lambda i: source_of(i) * tall + slot_of(i) // cut, lambda j: j))
+    inside = same((rows_all, MARK), lambda i: lax.rem(slot_of(i), cut), lambda j: j // tokens)
+    tile = one_hot(same((MARK, BLK), lambda i: lax.rem(i, tokens), lambda j: lax.rem(j, tokens)))
+    owner = same((rows_all, BLK), source_of, lambda j: j // tokens)
     total = jnp.zeros((), jnp.float32)
     for g in range(groups):
-        part = rall[g * batch : (g + 1) * batch].reshape(rows_main, -1)
-        marks = part[:, ff + BLK :]
-        pick = jnp.where(owner, dot_bf16(marks, tile_main), 0.0)
-        rest = jnp.where(owner, dot_bf16(marks, tile_extra), 0.0).astype(jnp.bfloat16)
-        rest = dot_bf16(chosen(0), rest)
-        total = total + jnp.sum(pick) + jnp.sum(rest)
-        base = g * rows_all
-        picks[base : base + rows_main, :] = pick.astype(jnp.bfloat16)
-        picks[base + rows_main : base + rows_all, :] = rest.astype(jnp.bfloat16)
-        gc[base : base + rows_main, :] = part[:, :ff]
-        for q in range(blocks):
-            spread = dot_bf16(chosen(q * extra), part[:, ff : ff + BLK])
-            gc[base + rows_main : base + rows_all, q * BLK : (q + 1) * BLK] = spread.astype(jnp.bfloat16)
+        marks = iall[g * batch : (g + 1) * batch].reshape(batch * tall, MARK)
+        marks = jnp.where(inside, dot_bf16(rise, marks), 0.0).astype(jnp.bfloat16)
+        pick = jnp.where(owner, dot_bf16(marks, tile), 0.0)
+        total = total + jnp.sum(pick)
+        picks[g * rows_all : (g + 1) * rows_all, :] = pick.astype(jnp.bfloat16)
 
     def select_rows(part):
         for g in range(groups):
@@ -623,37 +781,61 @@
     count_a = xc.shape[1] // BLK
     half = count_a // 2
 
-    def covariance(to, rows, damp):
+    def covariance(to, rows, level):
+        damp = 0.05 * jnp.exp(jnp.broadcast_to(0.4 * level.astype(jnp.float32), (1, BLK)))
         cov[to] = dot_bf16(rows, rows, TN) * scale + jnp.where(eye, damp, 0.0)
 
-    def slot(b):
-        return b + jnp.where(b >= half, blocks, 0)
-
+    def inverses(first, count, service):
+        invert(cov, first, count, work, tops, sides, quarter, side, mid, service)
+
+    def gradient(b, carry):
+        across = pl.multiple_of(b * BLK, BLK)
+        out_ref[pl.ds(across, BLK), :] = dot_bf16(xc[:, pl.ds(across, BLK)], gc[...], TN)
+        return carry
+
+    exchange.finish((0, 1))
     select_rows(0)
     select_rows(1)
     for b in range(half):
-        covariance(b, xc[:, b * BLK : (b + 1) * BLK], damp_a[b])
-    for b in range(blocks):
-        covariance(half + b, gc[:, b * BLK : (b + 1) * BLK], damp_f[b])
-    service()
-    invert(cov, 0, half + blocks, work, side, mid, service)
+        covariance(b, xc[:, b * BLK : (b + 1) * BLK], level_a[b])
+    inverses(0, half, service)
     while steps:
         service()
-    exchange.finish((2, 3))
+    for k in range(depth):
+        for part in late:
+            exchange.second(k, part)
+    exchange.wait_messages()
+    for g in range(groups):
+        part = rall[g * batch : (g + 1) * batch].reshape(rows_main, -1)
+        base = g * rows_all
+        gc[base : base + rows_main, :] = part[:, :ff]
+        for q in range(blocks):
+            chosen = one_hot(
+                same((rows_extra, rows_main), lambda i: (i // extra) * main + q * extra + lax.rem(i, extra), lambda j: j)
+            )
+            moved = dot_bf16(chosen, part[:, ff : ff + BLK])
+            gc[base + rows_main : base + rows_all, q * BLK : (q + 1) * BLK] = moved.astype(jnp.bfloat16)
+    for b in range(blocks):
+        covariance(count_a + b, gc[:, b * BLK : (b + 1) * BLK], level_f[b])
+    for k in range(depth):
+        for part in late:
+            exchange.third(k, part)
+    lax.fori_loop(0, half, gradient, 0)
+    exchange.finish(late)
     select_rows(2)
     select_rows(3)
     for b in range(half, count_a):
-        covariance(blocks + b, xc[:, b * BLK : (b + 1) * BLK], damp_a[b])
-    invert(cov, half + blocks, half, work, side, mid, service)
+        covariance(b, xc[:, b * BLK : (b + 1) * BLK], level_a[b])
+    inverses(half, half + blocks, None)
+    lax.fori_loop(half, count_a, gradient, 0)
 
     norm[...] = jnp.zeros_like(norm)
 
     def product(b, carry):
         across = pl.multiple_of(b * BLK, BLK)
-        gradient = dot_bf16(xc[:, pl.ds(across, BLK)], gc[...], TN)
-        left = split(cov[slot(b)], 2)
+        left = split(cov[b], 2)
         for c in range(blocks):
-            right = three(split(gradient[:, c * BLK : (c + 1) * BLK], 2), split(cov[half + c], 2))
+            right = three(split(out_ref[pl.ds(across, BLK), c * BLK : (c + 1) * BLK], 2), split(cov[count_a + c], 2))
             out = three(left, split(right, 2))
             out_ref[pl.ds(across, BLK), c * BLK : (c + 1) * BLK] = out
             norm[...] += jnp.sum((out * out).reshape(-1, 8, BLK), axis=0)
@@ -719,41 +901,6 @@
     return min(tok_rows, max(2, 5 * tok_rows // (2 * group_count)))
 
 
-def pack_messages(out_grad, expert_ids, group_count, shard_count, capacity, main):
-    tok_rows, _, ff_full = out_grad.shape
-    ff_dev = ff_full // shard_count
-    extra = capacity - main
-    total = group_count * shard_count
-    flat_ids = expert_ids.reshape(-1)
-    member = (flat_ids[:, None] == jnp.arange(group_count, dtype=jnp.int32)[None, :]).astype(jnp.int32)
-    before = jnp.cumsum(member, axis=0) - member
-    ranking = jnp.sum(before * member, axis=1)
-    target = flat_ids * capacity + ranking
-    dispatch = (jnp.arange(group_count * capacity, dtype=jnp.int32)[:, None] == target[None, :]).astype(jnp.bfloat16)
-    per_token = jnp.sum(dispatch.reshape(-1, tok_rows, 2).astype(jnp.float32), axis=2).astype(jnp.bfloat16)
-    sent = jnp.dot(dispatch, out_grad.reshape(2 * tok_rows, ff_full), preferred_element_type=jnp.float32)
-    sent = sent.astype(jnp.bfloat16).reshape(group_count, capacity, ff_full)
-    marks = per_token.reshape(group_count, capacity, tok_rows)
-    first = sent[:, :main].reshape(group_count, main, shard_count, ff_dev).transpose(0, 2, 1, 3)
-    last = sent[:, main:].reshape(group_count, extra, shard_count, ff_dev // BLK, BLK).transpose(0, 2, 3, 1, 4)
-    info = jnp.concatenate(
-        (
-            marks[:, :main],
-            jnp.pad(marks[:, main:], ((0, 0), (0, main - extra), (0, 0))),
-            jnp.zeros((group_count, main, MARK - 2 * tok_rows), jnp.bfloat16),
-        ),
-        axis=2,
-    )
-    return jnp.concatenate(
-        (
-            first.reshape(total, main, ff_dev),
-            last.reshape(total, main, BLK),
-            jnp.broadcast_to(info[:, None], (group_count, shard_count, main, MARK)).reshape(total, main, MARK),
-        ),
-        axis=2,
-    )
-
-
 def fast(tokens_in, out_grad, expert_ids, d_levels, f_levels):
     group_count = lax.axis_size("expert")
     shard_count = lax.axis_size("shard")
@@ -766,7 +913,8 @@
     main = 16 * (capacity // 16)
     total = group_count * shard_count
     depth = shard_count // (group_count // 2)
-    messages = pack_messages(out_grad, expert_ids, group_count, shard_count, capacity, main)
+    tall = capacity * tok_rows // MARK
+    tall += -tall % 8
     row_total = total * capacity
     count = count_a // 2 + blocks
     vmem = pl.BlockSpec(memory_space=pltpu.VMEM)
@@ -778,16 +926,22 @@
             pltpu.VMEM((width, ff_dev), f32),
             jax.ShapeDtypeStruct((8, 128), f32),
         ),
-        in_specs=[smem, smem, vmem, vmem],
+        in_specs=[smem, smem, vmem, vmem, vmem],
         out_specs=(vmem, vmem),
         scratch_shapes=[
+            pltpu.VMEM((total, main, ff_dev + BLK), bf16),
+            pltpu.VMEM((group_count, tall, MARK), bf16),
             pltpu.VMEM((4, total, tok_rows, width // 4), bf16),
-            pltpu.VMEM(messages.shape, bf16),
+            pltpu.VMEM((total, main, ff_dev + BLK), bf16),
+            pltpu.VMEM((total, tall, MARK), bf16),
             pltpu.VMEM((row_total, BLK), bf16),
             pltpu.VMEM((row_total, width), bf16),
             pltpu.VMEM((row_total, ff_dev), bf16),
             pltpu.VMEM((count_a + blocks, BLK, BLK), f32),
-            pltpu.VMEM((count // 2, LEAF, 128), f32),
+            pltpu.VMEM((count * LEAF // 128, LEAF, 128), f32),
+            pltpu.VMEM((count * LEAF // 128, LEAF, 128), f32),
+            pltpu.VMEM((count * LEAF // 128, LEAF, 128), f32),
+            pltpu.VMEM((count, HALF, HALF), f32),
             pltpu.VMEM((count, HALF, HALF), f32),
             pltpu.VMEM((count, HALF // 2, HALF // 2), f32),
             pltpu.VMEM((8, BLK), f32),
@@ -799,12 +953,20 @@
             dma((total,)),
             dma((4 * total,)),
             dma((total,)),
-            dma((5,)),
+            dma((6,)),
+            dma((total,)),
+            dma((total,)),
             dma((total,)),
             dma((total,)),
         ],
         compiler_params=pltpu.CompilerParams(collective_id=0, has_side_effects=True, vmem_limit_bytes=36 << 20),
-    )(damping(d_levels[0]), damping(f_levels[0]), tokens_in, messages)
+    )(
+        d_levels[0],
+        f_levels[0],
+        tokens_in,
+        out_grad.reshape(2 * tok_rows, ff_full),
+        expert_ids.reshape(1, 2 * tok_rows),
+    )
     ascent = pl.pallas_call(
         scale_kernel,
         out_shape=jax.ShapeDtypeStruct((width, ff_dev), bf16),
@@ -824,8 +986,8 @@
     main = 16 * (capacity_of(tok_rows, group_count) // 16)
     extra = capacity_of(tok_rows, group_count) - main
     chips = group_count // 2 == 2 and shard_count % 2 == 0
-    packed = main > 0 and extra * blocks == main and 2 * tok_rows <= MARK and BLK % tok_rows == 0
-    even = (group_count * shard_count * tok_rows) % BLK == 0 and width % (4 * BLK) == 0 and blocks % 2 == 0
+    packed = main > 0 and extra * blocks == main and MARK % tok_rows == 0 and (main + extra) % (MARK // tok_rows) == 0
+    even = (group_count * shard_count * tok_rows) % BLK == 0 and width % (8 * BLK) == 0 and blocks % 4 == 0
     small = group_count * shard_count * tok_rows * width * 2 <= 12 << 20
     if chips and packed and even and small:
         return fast(tokens_in, out_grad, expert_ids, d_levels, f_levels)

time: 178 us -> 159 us (0.89)
  Pallas kernels: 169 us -> 154 us
  other arithmetic: 2.67 us -> 0 us
    pallas_call x1, Pallas kernels: 165 us -> 150 us  [fast(): pl.pallas_call(functools.partial(fused_kernel, group_count, shard_count,...]
where the time goes in v3:
time: 159 us
  Pallas kernels  154 us (97%)
  local copies, waits for them, and re-layouts  4.58 us (3%)
    pallas_call x1, Pallas kernels, fast(): pl.pallas_call(functools.partial(fused_kernel, group_count, shard_count,...  150 us
    pallas_call x1, Pallas kernels, fast(): pl.pallas_call(scale_kernel, out_shape=jax.ShapeDtypeStruct((width, ff_de...  4.21 us

profile of v3, /device:TPU:0, one launch (start us, length us, event | category | flops | bytes accessed | tf_op | source)
XLA Modules:
  0.0 158.5 jit_solution(13476998588945107111)
XLA Ops:
  0.0 0.8 copy.7
  0.8 0.1 reshape.7.ids_ref
  0.9 1.5 reshape.6.g_ref
  2.3 0.0 copy-start
  2.4 0.9 copy-done
  3.3 0.0 copy-start.1
  3.3 0.7 copy-done.1
  4.0 0.0 copy-start.2
  4.0 0.7 copy-done.2
  4.6 149.5 %shard_map.55 = (f32[4096,1024]{1,0:T(8,128)S(1)}, f32[8,128]{1,0:T(8,128)S(1)}) custom-call(s32[16]{0:T(128)S(1)} %bitcast.3, s32[4]{0:T(128)S(1)} %bitcast.4, bf16[32,4096]{1,0:T(8,128)(2,1)S(1)} %copy-done, bf16[64,8192]{1,0:T(8,128)(2,1)S(1)} %reshape.6.g_ref, s32[1,64]{1,0:T(1,128)S(1)} %reshape.7.ids_ref), custom_call_target="tpu_custom_call" | custom-call | tf_op jit(solution)/shard_map/pallas_call | solution.py:923
  154.2 4.2 %shard_map.56 = bf16[4096,1024]{1,0:T(8,128)(2,1)} custom-call(f32[4096,1024]{1,0:T(8,128)S(1)} %get-tuple-element.7.value_ref, f32[8,128]{1,0:T(8,128)S(1)} %get-tuple-element.8.scale_ref), custom_call_target="tpu_custom_call" | custom-call | tf_op jit(solution)/shard_map/pallas_call | solution.py:970
Async XLA Ops:
  2.3 1.0 copy-start
  3.3 0.7 copy-start.1
  4.0 0.7 copy-start.2
